TPU v7x, 128 devices: a whole 4x4x4 slice. The times are simulated.
128 devices in a mesh: ty: 8 (over x, core), tx: 16 (over z, y).
Axes of the slice: x: 4, y: 4, z: 4, core: 2. Of those that a mesh axis runs over, the one named last changes fastest.
Arguments:
- exposures: float32 [1024, 128, 128], P(('ty', 'tx')), may hold values from -70 to 70
- point_spread: float32 [1024, 31, 31], P(('ty', 'tx')), may hold values from 0.0001 to 1
- warp_steps: int32 [1024, 2], P(('ty', 'tx')), may hold values from 0 to 3
- column: int32 [1024, 1], P(('ty', 'tx')), may hold values from 0 to 15; in each aligned block of 8 rows (0 to 7, 8 to 15, ...) at most 2 rows name the same one
- block_cell: int32 [1024], P(('ty', 'tx')), may hold values from 0 to 15
Outputs:
- solution: float32 [4096, 8192], P('ty', 'tx')
- residual: float32 [4096, 8192], P('ty', 'tx')
Inputs may be any that keep to these rules, and one draw needn't show every extreme that they name: `column`: among the 8 frame blocks of one device (aligned blocks of 8 rows) no value occurs more than 2 times, and in some such block one value occurs exactly 2 times.
All inputs are finite; a program needn't handle non-finite values.
Results may differ from a plain program's by a relative error of at most 0.0042.
Values may be sent and summed in bfloat16 or wider, within the bound.
No kernel may reach another device: no remote copies, remote signals or barrier semaphores. Data moves between devices by JAX's collectives and lax.ppermute only.
A program may use at most 192 MiB of HBM per device.

v0:
```python
import jax
import jax.numpy as jnp
from jax import lax
from jax.experimental import pallas as pl
from jax.experimental.pallas import tpu as pltpu
from jax.sharding import Mesh
from jax.sharding import PartitionSpec as P

TX = ("tx_0", "tx_1")
TY = ("ty_0", "ty_1")
TY_TX = TY + TX
N_TY, N_TX = 8, 16

SUB = 4
DAMPING = 0.05
FB = 8
CAP = 2
SLOTS = N_TX * CAP
TILE, BLOCK, HALO, TAPS, PSF = 512, 128, 16, 32, 31
EXT = TILE + 2 * HALO
LANES = 640
RIM = 2 * HALO
WIN = BLOCK + 2 * HALO
SLOT_ROWS = 160
GROUP = 4
F32, BF16 = jnp.float32, jnp.bfloat16
VMEM_BYTES = 38 << 20


def iota(shape, axis):
    return lax.broadcasted_iota(jnp.int32, shape, axis)


def by_group(lane, parts):
    low = jnp.where(lane < 32, parts[0], parts[1])
    high = jnp.where(lane < 96, parts[2], parts[3])
    return jnp.where(lane < 64, low, high)


def pack_kernel(labels, spread_ref, exposures_ref, out_ref, pad, kern):
    pad[...] = jnp.zeros_like(pad)
    for f in range(FB):
        pad[f, 0:PSF, 0:PSF] = spread_ref[:, f, :]
    for f in range(FB):
        point = pad[f]
        point = point / jnp.sum(point, keepdims=True)
        row_frac = labels[0, f].astype(F32) / SUB
        col_frac = labels[1, f].astype(F32) / SUB
        blended = (1.0 - col_frac) * point + col_frac * pltpu.roll(point, 1, 1)
        lowered = pltpu.roll(blended, 1, 0)
        kern[32 * f : 32 * f + 32, :] = (
            (1.0 - row_frac) * blended + row_frac * lowered
        ).astype(BF16)
    row, lane = iota((128, 128), 0), iota((128, 128), 1)
    tall, wide = iota((32 * FB, 128), 0), iota((32 * FB, 128), 1)
    tap = tall & 31
    place = jnp.where((lane & 31) == 31 - row, 1.0, 0.0).astype(BF16)
    spread = jnp.dot(kern[...], place, preferred_element_type=F32)
    spread = jnp.where((wide >> 5) == ((tap >> 2) & 3), spread, 0.0).astype(BF16)
    target, source = iota((8 * FB, 32 * FB), 0), iota((8 * FB, 32 * FB), 1)
    s_tap = source & 31
    pick = ((source >> 5) == (target >> 3)) & (
        (target & 7) == 2 * (s_tap & 3) + (s_tap >> 4)
    )
    backward = jnp.dot(
        jnp.where(pick, 1.0, 0.0).astype(BF16), spread, preferred_element_type=F32
    )
    place = jnp.where((lane & 63) == row, 1.0, 0.0).astype(BF16)
    spread = jnp.dot(kern[...], place, preferred_element_type=F32)
    spread = jnp.where((wide >> 6) == (tap & 1), spread, 0.0).astype(BF16)
    target, source = iota((16 * FB, 32 * FB), 0), iota((16 * FB, 32 * FB), 1)
    pick = ((source >> 5) == (target >> 4)) & ((target & 15) == ((source & 31) >> 1))
    ahead = jnp.dot(
        jnp.where(pick, 1.0, 0.0).astype(BF16), spread, preferred_element_type=F32
    )
    for s in range(SLOTS):
        out_ref[s, 128:SLOT_ROWS, :] = jnp.zeros((SLOT_ROWS - 128, 128), BF16)
    for f in range(FB):
        standing = jnp.int32(0)
        for g in range(f):
            standing = standing + jnp.where(labels[2, g] == labels[2, f], 1, 0)
        slot = CAP * labels[2, f] + jnp.minimum(standing, CAP - 1)
        out_ref[slot, 0:BLOCK, :] = exposures_ref[f].astype(BF16)
        tail = jnp.concatenate(
            [
                backward[8 * f : 8 * f + 8],
                ahead[16 * f : 16 * f + 16],
                jnp.broadcast_to((labels[3, f] + 1).astype(F32), (8, 128)),
            ],
            axis=0,
        )
        out_ref[slot, 128:SLOT_ROWS, :] = tail.astype(BF16)


def pack(labels, spread, exposures):
    smem = pl.BlockSpec(memory_space=pltpu.SMEM)
    vmem = pl.BlockSpec(memory_space=pltpu.VMEM)
    return pl.pallas_call(
        pack_kernel,
        out_shape=jax.ShapeDtypeStruct((SLOTS, SLOT_ROWS, 128), BF16),
        in_specs=[smem, vmem, vmem],
        out_specs=vmem,
        scratch_shapes=[pltpu.VMEM((FB, 32, 128), F32), pltpu.VMEM((32 * FB, 128), BF16)],
        compiler_params=pltpu.CompilerParams(vmem_limit_bytes=VMEM_BYTES),
        name="pack",
    )(labels, spread, exposures)


def list_frames(cells, frames):
    count = jnp.int32(0)
    for s in range(SLOTS):
        frames[count] = s
        count = count + jnp.where(cells[s] > 0, 1, 0)
    return count


def build_taps(taps, taps_out):
    row, lane = iota((64, 128), 0), iota((64, 128), 1)
    offset = (lane & 31) + 31 - row
    inside = (offset >= 0) & (offset < 32)
    for a2 in range(4):
        for h in range(2):
            line = jnp.broadcast_to(taps[2 * a2 + h : 2 * a2 + h + 1], (64, 128))
            line = pltpu.roll(line, 97, 1, stride=1, stride_axis=0)
            taps_out[0, 64 * a2 : 64 * a2 + 64, 128 * h : 128 * h + 128] = jnp.where(
                inside, line, 0.0
            ).astype(BF16)
    for a1 in range(8):
        for half in range(2):
            at = 8 + 2 * a1 + half
            line = jnp.broadcast_to(taps[at : at + 1], (32, 128))
            line = pltpu.roll(line, 0, 1, stride=1, stride_axis=0)
            taps_out[1, 32 * a1 : 32 * a1 + 32, 128 * half : 128 * half + 128] = line.astype(
                BF16
            )


def unfold(field, copies, doubled, stack):
    rows = 32
    source, target = iota((256, 512), 0), iota((256, 512), 1)
    copies[...] = jnp.where(source == 32 * (target >> 7) + (target & 63), 1.0, 0.0).astype(BF16)

    def columns(at, carry):
        both = pl.ds(pl.multiple_of(128 * at, 128), 256)
        wide = jnp.dot(field[:, both].astype(BF16), copies[...], preferred_element_type=F32)
        for k in range(4):
            doubled[k] = wide[:, 128 * k : 128 * k + 128]
        lane = iota((rows, 128), 1)
        for k in range(4):
            for r in range(0, EXT, rows):
                part = [doubled[k, r + a : r + a + rows] for a in range(4)]
                stack[4 * at + k, r : r + rows, 0:128] = jnp.where(
                    lane < 64, part[0], part[1]
                ).astype(BF16)
                stack[4 * at + k, r : r + rows, 128:256] = jnp.where(
                    lane < 64, part[2], part[3]
                ).astype(BF16)
        return carry

    lax.fori_loop(0, TILE // 128, columns, 0)


def fold(total, field):
    rows = 32
    lane = iota((rows, 128), 1)

    def block(b, r):
        even = total[b, r + 8 : r + 8 + rows, 0:128] + total[b, r + 6 : r + 6 + rows, 128:256]
        odd = total[b, r + 7 : r + 7 + rows, 0:128] + total[b, r + 5 : r + 5 + rows, 128:256]
        return jnp.where(lane < 64, even, odd)

    def columns(at, carry):
        here = pl.ds(pl.multiple_of(128 * at, 128), 128)
        for r in range(0, EXT, rows):
            before = block(4 * at, r)
            b0, b1, b2, b3 = [block(4 * at + 1 + k, r) for k in range(4)]
            even = jnp.where(lane < 64, b0, b2) + pltpu.roll(jnp.where(lane < 64, b2, b0), 64, 1)
            direct = jnp.where(lane < 64, b1, jnp.where(lane < 96, b3, before))
            turned = jnp.where(lane < 64, jnp.where(lane < 32, b3, before), b1)
            odd = pltpu.roll(direct, 32, 1) + pltpu.roll(turned, 96, 1)
            field[r : r + rows, here] = even + odd
        return carry

    lax.fori_loop(0, TILE // 128, columns, 0)
    for r in range(0, EXT, rows):
        before = block(TILE // 32, r)
        before = pltpu.roll(before, 32, 1) + pltpu.roll(before, 96, 1)
        field[r : r + rows, TILE:LANES] = jnp.where(lane < RIM, before, 0.0)


def clear_total(total):
    def clear(b, carry):
        total[b] = jnp.zeros(total.shape[1:], F32)
        return carry

    lax.fori_loop(0, total.shape[0], clear, 0)


def expand(image, turned, spread):
    for d in range(4):
        turned[d, 16:144] = image if d == 0 else pltpu.roll(image, 32 * d, 1)
    lane = iota((144, 128), 1)
    for xb in range(4):
        parts = [turned[(j - xb) % 4, 16 - 4 * j : 160 - 4 * j] for j in range(4)]
        spread[xb, 16:160] = by_group(lane, parts).astype(BF16)


def add_window(spread, taps, total, lx, top):
    both = jnp.concatenate([spread[:, 16:176], spread[:, 0:160]], axis=2).reshape(640, 256)
    window = jnp.dot(both, taps, preferred_element_type=F32).reshape(4, WIN, 256)
    at = pl.ds(pl.multiple_of(8 + top, 8), WIN)
    total[pl.ds(1 + lx, 4), at, :] += window


def clear_margins(turned, spread):
    for g in range(GROUP):
        turned[g, :, 0:16] = jnp.zeros((4, 16, 128), F32)
        turned[g, :, 144:160] = jnp.zeros((4, 16, 128), F32)
        spread[g, :, 0:16] = jnp.zeros((4, 16, 128), BF16)
        spread[g, :, 160:176] = jnp.zeros((4, 16, 128), BF16)


def over_frames(count, step, carry):
    groups = count // GROUP

    def group(k, carry):
        return step([GROUP * k + g for g in range(GROUP)], carry)

    carry = lax.fori_loop(0, groups, group, carry)
    return lax.fori_loop(GROUP * groups, count, lambda i, carry: step([i], carry), carry)


def place_of(cells, frames, i):
    cell = cells[frames[i]] - 1
    return 4 * (cell & 3), BLOCK * (cell >> 2)


def write_rims(place, field, first_ref, second_ref, top_ref, bottom_ref):
    first_ref[...] = jnp.zeros_like(first_ref)
    second_ref[...] = jnp.zeros_like(second_ref)
    even = (place[1] & 1) == 0
    for r in range(0, EXT, 128):
        n = min(128, EXT - r)
        left = field[r : r + n, 0:128].T[0:RIM]
        right = field[r : r + n, TILE : TILE + 128].T[0:RIM]
        first_ref[:, r : r + n] = jnp.where(even, right, left)
        second_ref[:, r : r + n] = jnp.where(even, left, right)
    top_ref[...] = field[0:RIM, :]
    bottom_ref[...] = field[TILE:EXT, :]


def neighbours(index, size, first, second):
    even = (index & 1) == 0
    before = jnp.where(even, second, first)
    after = jnp.where(even, first, second)
    before = jnp.where(index > 0, before, 0.0)
    after = jnp.where(index < size - 1, after, 0.0)
    return before, after


def complete(place, own, rims, field):
    field[0:EXT, :] = own[...]
    field[EXT:, :] = jnp.zeros((field.shape[0] - EXT, LANES), F32)
    for r in range(0, EXT, 128):
        n = min(128, EXT - r)
        lanes = slice(r, r + 128)
        left, right = neighbours(place[1], N_TX, rims[0][:, lanes], rims[1][:, lanes])
        field[r : r + n, 0:RIM] += left.T[0:n]
        field[r : r + n, TILE:EXT] += right.T[0:n]
    above, below = neighbours(place[0], N_TY, rims[2][...], rims[3][...])
    field[0:RIM, :] += above
    field[TILE:EXT, :] += below

    @pl.when(place[0] == 0)
    def _():
        field[0:HALO, :] = jnp.zeros((HALO, LANES), F32)

    @pl.when(place[0] == N_TY - 1)
    def _():
        field[EXT - HALO : EXT, :] = jnp.zeros((HALO, LANES), F32)

    @pl.when(place[1] == 0)
    def _():
        field[0:EXT, 0:HALO] = jnp.zeros((EXT, HALO), F32)

    @pl.when(place[1] == N_TX - 1)
    def _():
        field[0:EXT, EXT - HALO : EXT] = jnp.zeros((EXT, HALO), F32)


def inner_sum(chunk_of):
    sums = jnp.zeros((1, 128), F32)
    lane = iota((32, LANES), 1)
    inside = (lane >= HALO) & (lane < HALO + TILE)
    for r in range(HALO, HALO + TILE, 32):
        chunk = jnp.where(inside, chunk_of(r, 32), 0.0)
        by_lane = jnp.sum(chunk, axis=0, keepdims=True)
        for x in range(0, LANES, 128):
            sums = sums + by_lane[:, x : x + 128]
    return sums


def first_kernel(
    cells, place, slots_ref, own_ref, left_ref, right_ref, top_ref, bottom_ref, taps_out,
    frames, taps, total, turned, spread, sems,
):
    count = list_frames(cells, frames)
    clear_total(total)
    clear_margins(turned, spread)

    def step(group, carry):
        for i in group:
            build_taps(slots_ref[frames[i], 128:SLOT_ROWS].astype(F32), taps.at[i])
            pltpu.make_async_copy(taps.at[i], taps_out.at[i], sems.at[i]).start()
        for g, i in enumerate(group):
            image = slots_ref[frames[i], 0:BLOCK].astype(F32)
            expand(image, turned.at[g], spread.at[g])
        for g, i in enumerate(group):
            add_window(spread.at[g], taps[i, 1], total, *place_of(cells, frames, i))
        return carry

    over_frames(count, step, 0)
    fold(total, own_ref)
    write_rims(place, own_ref, left_ref, right_ref, top_ref, bottom_ref)

    def wait(i, carry):
        pltpu.make_async_copy(taps.at[i], taps_out.at[i], sems.at[i]).wait()
        return carry

    lax.fori_loop(0, count, wait, 0)


def frame_pass(cells, frames, count, taps_in, field, scratch):
    taps, total, turned, spread, stack, copies, doubled, product, paired, sems = scratch
    unfold(field, copies, doubled, stack)
    clear_total(total)
    clear_margins(turned, spread)

    def step(group, sums):
        for i in group:
            pltpu.make_async_copy(taps_in.at[i], taps.at[i], sems.at[i]).wait()
        for g, i in enumerate(group):
            lx, top = place_of(cells, frames, i)
            window = stack[pl.ds(lx, 4), pl.ds(pl.multiple_of(top, 128), WIN), :]
            product[g] = jnp.dot(
                window.reshape(4 * WIN, 256), taps[i, 0], preferred_element_type=F32
            ).reshape(4, WIN, 256)
        images = []
        for g in range(len(group)):
            for xb in range(4):
                paired[g, xb] = product[g, xb, 0:144, 0:128] + product[g, xb, 16:160, 128:256]
            lane = iota((BLOCK, 128), 1)
            modelled = None
            for d in range(4):
                parts = [paired[g, (j + d) % 4, 4 * j : 4 * j + BLOCK] for j in range(4)]
                moved = by_group(lane, parts)
                moved = moved if d == 0 else pltpu.roll(moved, 32 * d, 1)
                modelled = moved if d == 0 else modelled + moved
            image = modelled.astype(BF16).astype(F32)
            sums = sums + jnp.sum(modelled * image, axis=0, keepdims=True)
            images.append(image)
        for g, image in enumerate(images):
            expand(image, turned.at[g], spread.at[g])
        for g, i in enumerate(group):
            add_window(spread.at[g], taps[i, 1], total, *place_of(cells, frames, i))
        return sums

    return over_frames(count, step, jnp.zeros((1, 128), F32))


def start_taps(cells, frames, taps_in, taps, sems):
    count = list_frames(cells, frames)

    def start(i, carry):
        pltpu.make_async_copy(taps_in.at[i], taps.at[i], sems.at[i]).start()
        return carry

    lax.fori_loop(0, count, start, 0)
    return count


def second_kernel(
    cells, place, own_in, rim_l, rim_r, rim_a, rim_b, taps_in,
    own_ref, left_ref, right_ref, top_ref, bottom_ref, residual_ref, sums_ref,
    frames, field, *scratch,
):
    count = start_taps(cells, frames, taps_in, scratch[0], scratch[-1])
    complete(place, own_in, (rim_l, rim_r, rim_a, rim_b), field)
    residual_ref[...] = field[0:EXT, :]
    square = inner_sum(lambda r, n: field[r : r + n, :] * field[r : r + n, :])
    curve = frame_pass(cells, frames, count, taps_in, field, scratch)
    fold(scratch[1], own_ref)
    write_rims(place, own_ref, left_ref, right_ref, top_ref, bottom_ref)
    sums_ref[...] = jnp.zeros_like(sums_ref)
    sums_ref[0:1] = square
    sums_ref[1:2] = curve


def first_step(sums):
    square = jnp.sum(sums[0:1], axis=1, keepdims=True)
    curve = jnp.sum(sums[1:2], axis=1, keepdims=True) + DAMPING * square
    return square, curve, square / curve


def third_kernel(
    cells, place, sums_in, own_in, rim_l, rim_r, rim_a, rim_b, start_ref, taps_in,
    own_ref, left_ref, right_ref, top_ref, bottom_ref, residual_ref, applied_ref, sums_ref,
    frames, field, *scratch,
):
    count = start_taps(cells, frames, taps_in, scratch[0], scratch[-1])
    complete(place, own_in, (rim_l, rim_r, rim_a, rim_b), field)
    step = first_step(sums_in[...])[2]
    for r in range(0, EXT, 32):
        start = start_ref[r : r + 32]
        applied = field[r : r + 32, :] + DAMPING * start
        residual = start - step * applied
        applied_ref[r : r + 32] = applied
        residual_ref[r : r + 32] = residual
        field[r : r + 32, :] = residual
    square = inner_sum(lambda r, n: field[r : r + n, :] * field[r : r + n, :])
    cross = inner_sum(lambda r, n: field[r : r + n, :] * applied_ref[r : r + n, :])
    curve = frame_pass(cells, frames, count, taps_in, field, scratch)
    fold(scratch[1], own_ref)
    write_rims(place, own_ref, left_ref, right_ref, top_ref, bottom_ref)
    sums_ref[...] = jnp.zeros_like(sums_ref)
    sums_ref[0:1] = square
    sums_ref[1:2] = cross
    sums_ref[2:3] = curve


def last_kernel(
    place, sums_one, sums_two, own_in, rim_l, rim_r, rim_a, rim_b, start_ref, applied_ref,
    residual_ref, solution_out, residual_out, field,
):
    complete(place, own_in, (rim_l, rim_r, rim_a, rim_b), field)
    square_one, curve_one, step_one = first_step(sums_one[...])
    sums = sums_two[...]
    square_two = jnp.sum(sums[0:1], axis=1, keepdims=True)
    cross = jnp.sum(sums[1:2], axis=1, keepdims=True)
    curve = jnp.sum(sums[2:3], axis=1, keepdims=True) + DAMPING * square_two
    ratio = square_two / square_one
    curve_two = curve + 2.0 * ratio * cross + ratio * ratio * curve_one
    step_two = square_two / curve_two
    lane = iota((32, 128), 1)
    for r in range(0, TILE, 32):
        rows = slice(r + HALO, r + HALO + 32)
        start, residual = start_ref[rows], residual_ref[rows]
        applied = field[rows, :] + DAMPING * residual + ratio * applied_ref[rows]
        total = step_one * start + step_two * (residual + ratio * start)
        left = residual - step_two * applied
        for value, out in ((total, solution_out), (left, residual_out)):
            parts = [
                pltpu.roll(value[:, x : x + 128], 128 - HALO, 1) for x in range(0, LANES, 128)
            ]
            for x in range(TILE // 128):
                out[r : r + 32, 128 * x : 128 * x + 128] = jnp.where(
                    lane < 128 - HALO, parts[x], parts[x + 1]
                )


def corner_kernel(place, top_ref, bottom_ref, first_in, second_in, *rest):
    first_out, second_out, top, bottom = rest[-4:]
    top[...] = top_ref[...]
    bottom[...] = bottom_ref[...]
    left, right = neighbours(place[1], N_TX, first_in[...], second_in[...])
    for rim, at in ((left, 0), (right, TILE)):
        top[:, at : at + RIM] += rim[:, 0:128].T[0:RIM]
        bottom[:, at : at + RIM] += rim[:, TILE:LANES].T[0:RIM]
    even = (place[0] & 1) == 0
    first_out[...] = jnp.where(even, bottom[...], top[...])
    second_out[...] = jnp.where(even, top[...], bottom[...])


def call(kernel, outs, spaces, operands, scratch, name, out_spaces=None):
    specs = {
        "s": pl.BlockSpec(memory_space=pltpu.SMEM),
        "v": pl.BlockSpec(memory_space=pltpu.VMEM),
        "a": pl.BlockSpec(memory_space=pl.ANY),
    }
    return pl.pallas_call(
        kernel,
        out_shape=[jax.ShapeDtypeStruct(shape, kind) for shape, kind in outs],
        in_specs=[specs[space] for space in spaces],
        out_specs=[specs[space] for space in (out_spaces or "v" * len(outs))],
        scratch_shapes=scratch,
        compiler_params=pltpu.CompilerParams(vmem_limit_bytes=VMEM_BYTES),
        name=name,
    )(*operands)


FIELD = ((EXT, LANES), F32)
RIM_ARRAY = ((RIM, LANES), F32)
SUMS = ((8, 128), F32)
FRAME_LIST = pltpu.SMEM((SLOTS + 1,), jnp.int32)
TAPS_SCRATCH = pltpu.VMEM((SLOTS, 2, 256, 256), BF16)
TOTAL = pltpu.VMEM((TILE // 32 + 1, 8 + EXT, 256), F32)
TURNED = pltpu.VMEM((GROUP, 4, WIN, 128), F32)
SPREAD = pltpu.VMEM((GROUP, 4, WIN + 16, 128), BF16)
FIELD_SCRATCH = pltpu.VMEM((EXT + 8, LANES), F32)
PASS_SCRATCH = [
    FRAME_LIST,
    FIELD_SCRATCH,
    TAPS_SCRATCH,
    TOTAL,
    TURNED,
    SPREAD,
    pltpu.VMEM((TILE // 32, EXT, 256), BF16),
    pltpu.VMEM((256, 512), BF16),
    pltpu.VMEM((4, EXT + 8, 128), F32),
    pltpu.VMEM((GROUP, 4, WIN, 256), F32),
    pltpu.VMEM((GROUP, 4, 144, 128), F32),
    pltpu.SemaphoreType.DMA((SLOTS,)),
]


def trade(first, second, axes, size):
    near = [(i, i ^ 1) for i in range(size)]
    far = [(i, ((i + 1) ^ 1) - 1) for i in range(1, size - 1)] + [(0, size - 1), (size - 1, 0)]
    return lax.ppermute(first, axes, near), lax.ppermute(second, axes, far)


def sum_pairs(value, axis):
    value = value + lax.ppermute(value, axis, [(0, 1), (1, 0), (2, 3), (3, 2)])
    return value + lax.ppermute(value, axis, [(1, 2), (2, 1), (3, 0), (0, 3)])


def trade_rims(place, left, right, top, bottom, sums=None):
    rims = trade(left, right, TX, N_TX)
    ahead = ()
    if sums is not None:
        sums = sum_pairs(sums, "tx_1")
        ahead = (sums,)
    rows = call(
        corner_kernel,
        [RIM_ARRAY, RIM_ARRAY],
        "svvvv" + "a" * len(ahead),
        (place, top, bottom, *rims, *ahead),
        [pltpu.VMEM((RIM, LANES), F32)] * 2,
        "corners",
    )
    rims = (*rims, *trade(*rows, TY, N_TY))
    if sums is not None:
        sums = sums + lax.ppermute(sums, "ty_1", [(0, 1), (1, 0)])
        sums = sum_pairs(sum_pairs(sums, "tx_0"), "ty_0")
    return rims, sums


def body(exposures, point_spread, warp_steps, column, block_cell):
    place = jnp.stack([lax.axis_index(TY), lax.axis_index(TX)]).astype(jnp.int32)
    labels = jnp.concatenate([warp_steps.T, column.T, block_cell[None]])
    sent = pack(labels, point_spread.transpose(1, 0, 2), exposures)
    slots = lax.all_to_all(
        sent.reshape(N_TX, CAP, SLOT_ROWS, 128), TX, split_axis=0, concat_axis=0, tiled=True
    ).reshape(SLOTS, SLOT_ROWS, 128)
    cells = slots[:, SLOT_ROWS - 8, 0].astype(jnp.int32)
    rims_out = [RIM_ARRAY] * 4

    own, left, right, top, bottom, taps = call(
        first_kernel,
        [FIELD] + rims_out + [((SLOTS, 2, 256, 256), BF16)],
        "ssv",
        (cells, place, slots),
        [FRAME_LIST, TAPS_SCRATCH, TOTAL, TURNED, SPREAD, pltpu.SemaphoreType.DMA((SLOTS,))],
        "right_side",
        "vvvvva",
    )
    rims, _ = trade_rims(place, left, right, top, bottom)
    own, left, right, top, bottom, start, sums_one = call(
        second_kernel,
        [FIELD] + rims_out + [FIELD, SUMS],
        "ssvvvvva",
        (cells, place, own, *rims, taps),
        PASS_SCRATCH,
        "first_pass",
    )
    rims, sums_one = trade_rims(place, left, right, top, bottom, sums_one)
    own, left, right, top, bottom, residual, applied, sums_two = call(
        third_kernel,
        [FIELD] + rims_out + [FIELD, FIELD, SUMS],
        "ssvvvvvvva",
        (cells, place, sums_one, own, *rims, start, taps),
        PASS_SCRATCH,
        "second_pass",
    )
    rims, sums_two = trade_rims(place, left, right, top, bottom, sums_two)
    tile = ((TILE, TILE), F32)
    return tuple(
        call(
            last_kernel,
            [tile, tile],
            "svvvvvvvvvv",
            (place, sums_one, sums_two, own, *rims, start, applied, residual),
            [FIELD_SCRATCH],
            "finish",
        )
    )


def solution(mesh):
    torus = Mesh(mesh.devices.reshape(4, 2, 4, 4), TY_TX)
    in_specs = (
        P(TY_TX, None, None),
        P(TY_TX, None, None),
        P(TY_TX, None),
        P(TY_TX, None),
        P(TY_TX),
    )
    out_specs = (P(TY, TX), P(TY, TX))
    return jax.shard_map(body, mesh=torus, in_specs=in_specs, out_specs=out_specs, check_vma=False)
```

profile of v0, /device:TPU:0, one launch (start us, length us, event | category | flops | bytes accessed | tf_op | source)
XLA Modules:
  0.0 155.6 jit_solution(5419596879010727940)
XLA Ops:
  0.6 0.7 pad_add_fusion.labels
  1.4 1.0 copy-done
  2.4 0.9 copy-done.1
  3.3 2.4 %pack.1 = bf16[32,160,128]{2,1,0:T(8,128)(2,1)} custom-call(s32[4,8]{1,0:T(4,128)S(1)} %pad_add_fusion.labels, f32[31,8,31]{2,1,0:T(8,128)S(1)} %bitcast.10, f32[8,128,128]{2,1,0:T(8,128)S(1)} %copy-done), custom_call_target="tpu_custom_call" | custom-call | tf_op jit(solution)/shard_map/pack/pallas_call | solution.py:98
  5.7 8.1 %all-to-all-start = ((bf16[16,2,160,128]{3,2,1,0:T(8,128)(2,1)}), bf16[16,2,160,128]{3,2,1,0:T(8,128)(2,1)S(1)}, u32[]{:S(2)}, u32[]{:S(2)}) async-start(bf16[16,2,160,128]{3,2,1,0:T(8,128)(2,1)} %bitcast.6), calls=%async_computation | async-start | bytes 2621440 | tf_op jit(solution)/shard_map/all_to_all | solution.py:552
  13.9 20.7 %all-to-all-done = bf16[16,2,160,128]{3,2,1,0:T(8,128)(2,1)S(1)} async-done(((bf16[16,2,160,128]{3,2,1,0:T(8,128)(2,1)}), bf16[16,2,160,128]{3,2,1,0:T(8,128)(2,1)S(1)}, u32[]{:S(2)}, u32[]{:S(2)}) %all-to-all-start) | async-done | bytes 1310752 | tf_op jit(solution)/shard_map/all_to_all | solution.py:552
  34.7 0.7 fusion.cells
  35.3 6.8 %right_side.1 = (f32[544,640]{1,0:T(8,128)S(1)}, f32[32,640]{1,0:T(8,128)S(1)}, f32[32,640]{1,0:T(8,128)S(1)}, f32[32,640]{1,0:T(8,128)S(1)}, f32[32,640]{1,0:T(...) custom-call(s32[32]{0:T(128)S(1)} %fusion.cells, s32[2]{0:T(128)S(1)} %pad_add_fusion.1.place, bf16[32,160,128]{2,1,0:T(8,128)(2,1)S(1)} %bitcast.9), custom_call_target="tpu_custom_call" | custom-call | tf_op jit(solution)/shard_map/right_side/pallas_call | solution.py:480
  42.3 2.2 %collective-permute-start.1 = (f32[32,640]{1,0:T(8,128)S(1)}, f32[32,640]{1,0:T(8,128)S(1)}, u32[]{:S(2)}, u32[]{:S(2)}) collective-permute-start(f32[32,640]{1,0:T(8,128)S(1)} %get-tuple-element.31), channel_id=1, source_target_pairs={{1,2},{2,1},{3,4},{4,3},{5,6},{6,5},{7,8},{8,7},{9,10},{10,9},{11,... | collective-permute-start | bytes 245768 | tf_op jit(solution)/shard_map/ppermute | solution.py:519
  44.4 2.3 %collective-permute-done.first_in.rim_l = f32[32,640]{1,0:T(8,128)S(1)} collective-permute-done((f32[32,640]{1,0:T(8,128)S(1)}, f32[32,640]{1,0:T(8,128)S(1)}, u32[]{:S(2)}, u32[]{:S(2)}) %collective-permute-start) | collective-permute-done | bytes 81952 | tf_op jit(solution)/shard_map/ppermute | solution.py:519
  46.7 3.4 %collective-permute-done.1.second_in.rim_r = f32[32,640]{1,0:T(8,128)S(1)} collective-permute-done((f32[32,640]{1,0:T(8,128)S(1)}, f32[32,640]{1,0:T(8,128)S(1)}, u32[]{:S(2)}, u32[]{:S(2)}) %collective-permute-start.1) | collective-permute-done | bytes 81952 | tf_op jit(solution)/shard_map/ppermute | solution.py:519
  50.1 0.6 corners.3
  50.8 2.5 %collective-permute-start.3 = (f32[32,640]{1,0:T(8,128)S(1)}, f32[32,640]{1,0:T(8,128)S(1)}, u32[]{:S(2)}, u32[]{:S(2)}) collective-permute-start(f32[32,640]{1,0:T(8,128)S(1)} %get-tuple-element.35), channel_id=1, source_target_pairs={{16,32},{32,16},{48,64},{64,48},{80,96},{96,80},{0,112},{112,0},{1... | collective-permute-start | bytes 245768 | tf_op jit(solution)/shard_map/ppermute | solution.py:519
  53.3 2.7 %collective-permute-done.3.rim_b = f32[32,640]{1,0:T(8,128)S(1)} collective-permute-done((f32[32,640]{1,0:T(8,128)S(1)}, f32[32,640]{1,0:T(8,128)S(1)}, u32[]{:S(2)}, u32[]{:S(2)}) %collective-permute-start.3) | collective-permute-done | bytes 81952 | tf_op jit(solution)/shard_map/ppermute | solution.py:519
  56.0 10.0 %first_pass.1 = (f32[544,640]{1,0:T(8,128)S(1)}, f32[32,640]{1,0:T(8,128)S(1)}, f32[32,640]{1,0:T(8,128)S(1)}, f32[32,640]{1,0:T(8,128)S(1)}, f32[32,640]{1,0:T(...) custom-call(s32[32]{0:T(128)S(1)} %fusion.cells, s32[2]{0:T(128)S(1)} %pad_add_fusion.1.place, ...), custom_call_target="tpu_custom_call" | custom-call | tf_op jit(solution)/shard_map/first_pass/pallas_call | solution.py:480
  66.0 1.5 collective-permute-start.12
  67.6 0.5 collective-permute-start.4
  68.1 3.1 %collective-permute-done.4 = f32[8,128]{1,0:T(8,128)S(1)} collective-permute-done((f32[8,128]{1,0:T(8,128)S(1)}, f32[8,128]{1,0:T(8,128)S(1)}, u32[]{:S(2)}, u32[]{:S(2)}) %collective-permute-start.4) | collective-permute-done | bytes 4128 | tf_op jit(solution)/shard_map/ppermute | solution.py:523
  71.2 5.9 %collective-permute-start.5 = (f32[8,128]{1,0:T(8,128)S(1)}, f32[8,128]{1,0:T(8,128)S(1)}, u32[]{:S(2)}, u32[]{:S(2)}) collective-permute-start(f32[8,128]{1,0:T(8,128)S(1)} %add.50), channel_id=1, source_target_pairs={{1,2},{2,1},{3,0},{0,3},{5,6},{6,5},{7,4},{4,7},{9,10},{10,9},{11,... | collective-permute-start | bytes 12296 | tf_op jit(solution)/shard_map/ppermute | solution.py:524
  77.1 1.6 %collective-permute-done.5 = f32[8,128]{1,0:T(8,128)S(1)} collective-permute-done((f32[8,128]{1,0:T(8,128)S(1)}, f32[8,128]{1,0:T(8,128)S(1)}, u32[]{:S(2)}, u32[]{:S(2)}) %collective-permute-start.5) | collective-permute-done | bytes 4128 | tf_op jit(solution)/shard_map/ppermute | solution.py:524
  78.7 0.6 corners.4
  79.4 3.3 %collective-permute-start.14 = (f32[32,640]{1,0:T(8,128)S(1)}, f32[32,640]{1,0:T(8,128)S(1)}, u32[]{:S(2)}, u32[]{:S(2)}) collective-permute-start(f32[32,640]{1,0:T(8,128)S(1)} %get-tuple-element.44), channel_id=1, source_target_pairs={{16,32},{32,16},{48,64},{64,48},{80,96},{96,80},{0,112},{112,0},{1... | collective-permute-start | bytes 245768 | tf_op jit(solution)/shard_map/ppermute | solution.py:519
  82.7 1.2 collective-permute-done.6
  83.9 6.8 %collective-permute-start.7 = (f32[8,128]{1,0:T(8,128)S(1)}, f32[8,128]{1,0:T(8,128)S(1)}, u32[]{:S(2)}, u32[]{:S(2)}) collective-permute-start(f32[8,128]{1,0:T(8,128)S(1)} %add.52), channel_id=1, source_target_pairs={{0,4},{4,0},{8,12},{12,8},{1,5},{5,1},{9,13},{13,9},{2,6},{6,2},{1... | collective-permute-start | bytes 12296 | tf_op jit(solution)/shard_map/ppermute | solution.py:523
  90.6 1.6 %collective-permute-done.7 = f32[8,128]{1,0:T(8,128)S(1)} collective-permute-done((f32[8,128]{1,0:T(8,128)S(1)}, f32[8,128]{1,0:T(8,128)S(1)}, u32[]{:S(2)}, u32[]{:S(2)}) %collective-permute-start.7) | collective-permute-done | bytes 4128 | tf_op jit(solution)/shard_map/ppermute | solution.py:523
  92.2 4.6 %collective-permute-start.8 = (f32[8,128]{1,0:T(8,128)S(1)}, f32[8,128]{1,0:T(8,128)S(1)}, u32[]{:S(2)}, u32[]{:S(2)}) collective-permute-start(f32[8,128]{1,0:T(8,128)S(1)} %add.53), channel_id=1, source_target_pairs={{4,8},{8,4},{12,0},{0,12},{5,9},{9,5},{13,1},{1,13},{6,10},{10,6},... | collective-permute-start | bytes 12296 | tf_op jit(solution)/shard_map/ppermute | solution.py:524
  96.8 1.6 %collective-permute-done.8 = f32[8,128]{1,0:T(8,128)S(1)} collective-permute-done((f32[8,128]{1,0:T(8,128)S(1)}, f32[8,128]{1,0:T(8,128)S(1)}, u32[]{:S(2)}, u32[]{:S(2)}) %collective-permute-start.8) | collective-permute-done | bytes 4128 | tf_op jit(solution)/shard_map/ppermute | solution.py:524
  98.9 3.1 %collective-permute-done.9 = f32[8,128]{1,0:T(8,128)S(1)} collective-permute-done((f32[8,128]{1,0:T(8,128)S(1)}, f32[8,128]{1,0:T(8,128)S(1)}, u32[]{:S(2)}, u32[]{:S(2)}) %collective-permute-start.9) | collective-permute-done | bytes 4128 | tf_op jit(solution)/shard_map/ppermute | solution.py:523
  102.0 1.4 collective-permute-start.10
  103.5 3.4 %collective-permute-done.10 = f32[8,128]{1,0:T(8,128)S(1)} collective-permute-done((f32[8,128]{1,0:T(8,128)S(1)}, f32[8,128]{1,0:T(8,128)S(1)}, u32[]{:S(2)}, u32[]{:S(2)}) %collective-permute-start.10) | collective-permute-done | bytes 4128 | tf_op jit(solution)/shard_map/ppermute | solution.py:524
  106.9 10.7 %second_pass.1 = (f32[544,640]{1,0:T(8,128)S(1)}, f32[32,640]{1,0:T(8,128)S(1)}, f32[32,640]{1,0:T(8,128)S(1)}, f32[32,640]{1,0:T(8,128)S(1)}, f32[32,640]{1,0:T...) custom-call(s32[32]{0:T(128)S(1)} %fusion.cells, s32[2]{0:T(128)S(1)} %pad_add_fusion.1.place, ...), custom_call_target="tpu_custom_call" | custom-call | tf_op jit(solution)/shard_map/second_pass/pallas_call | solution.py:480
  117.6 1.9 %collective-permute-start.23 = (f32[32,640]{1,0:T(8,128)S(1)}, f32[32,640]{1,0:T(8,128)S(1)}, u32[]{:S(2)}, u32[]{:S(2)}) collective-permute-start(f32[32,640]{1,0:T(8,128)S(1)} %get-tuple-element.49), channel_id=1, source_target_pairs={{1,2},{2,1},{3,4},{4,3},{5,6},{6,5},{7,8},{8,7},{9,10},{10,9},{11,... | collective-permute-start | bytes 245768 | tf_op jit(solution)/shard_map/ppermute | solution.py:519
  119.5 0.5 collective-permute-start.15
  120.0 3.1 %collective-permute-done.15 = f32[8,128]{1,0:T(8,128)S(1)} collective-permute-done((f32[8,128]{1,0:T(8,128)S(1)}, f32[8,128]{1,0:T(8,128)S(1)}, u32[]{:S(2)}, u32[]{:S(2)}) %collective-permute-start.15) | collective-permute-done | bytes 4128 | tf_op jit(solution)/shard_map/ppermute | solution.py:523
  123.1 2.3 %collective-permute-start.16 = (f32[8,128]{1,0:T(8,128)S(1)}, f32[8,128]{1,0:T(8,128)S(1)}, u32[]{:S(2)}, u32[]{:S(2)}) collective-permute-start(f32[8,128]{1,0:T(8,128)S(1)} %add.57), channel_id=1, source_target_pairs={{1,2},{2,1},{3,0},{0,3},{5,6},{6,5},{7,4},{4,7},{9,10},{10,9},{11,... | collective-permute-start | bytes 12296 | tf_op jit(solution)/shard_map/ppermute | solution.py:524
  125.4 2.5 %collective-permute-done.16 = f32[8,128]{1,0:T(8,128)S(1)} collective-permute-done((f32[8,128]{1,0:T(8,128)S(1)}, f32[8,128]{1,0:T(8,128)S(1)}, u32[]{:S(2)}, u32[]{:S(2)}) %collective-permute-start.16) | collective-permute-done | bytes 4128 | tf_op jit(solution)/shard_map/ppermute | solution.py:524
  127.9 0.6 corners.5
  128.7 3.2 %collective-permute-start.25 = (f32[32,640]{1,0:T(8,128)S(1)}, f32[32,640]{1,0:T(8,128)S(1)}, u32[]{:S(2)}, u32[]{:S(2)}) collective-permute-start(f32[32,640]{1,0:T(8,128)S(1)} %get-tuple-element.53), channel_id=1, source_target_pairs={{16,32},{32,16},{48,64},{64,48},{80,96},{96,80},{0,112},{112,0},{1... | collective-permute-start | bytes 245768 | tf_op jit(solution)/shard_map/ppermute | solution.py:519
  131.9 1.2 collective-permute-done.17
  133.0 3.3 %collective-permute-start.18 = (f32[8,128]{1,0:T(8,128)S(1)}, f32[8,128]{1,0:T(8,128)S(1)}, u32[]{:S(2)}, u32[]{:S(2)}) collective-permute-start(f32[8,128]{1,0:T(8,128)S(1)} %add.59), channel_id=1, source_target_pairs={{0,4},{4,0},{8,12},{12,8},{1,5},{5,1},{9,13},{13,9},{2,6},{6,2},{1... | collective-permute-start | bytes 12296 | tf_op jit(solution)/shard_map/ppermute | solution.py:523
  136.3 1.6 %collective-permute-done.18 = f32[8,128]{1,0:T(8,128)S(1)} collective-permute-done((f32[8,128]{1,0:T(8,128)S(1)}, f32[8,128]{1,0:T(8,128)S(1)}, u32[]{:S(2)}, u32[]{:S(2)}) %collective-permute-start.18) | collective-permute-done | bytes 4128 | tf_op jit(solution)/shard_map/ppermute | solution.py:523
  137.9 4.6 %collective-permute-start.19 = (f32[8,128]{1,0:T(8,128)S(1)}, f32[8,128]{1,0:T(8,128)S(1)}, u32[]{:S(2)}, u32[]{:S(2)}) collective-permute-start(f32[8,128]{1,0:T(8,128)S(1)} %add.60), channel_id=1, source_target_pairs={{4,8},{8,4},{12,0},{0,12},{5,9},{9,5},{13,1},{1,13},{6,10},{10,6},... | collective-permute-start | bytes 12296 | tf_op jit(solution)/shard_map/ppermute | solution.py:524
  142.5 1.6 %collective-permute-done.19 = f32[8,128]{1,0:T(8,128)S(1)} collective-permute-done((f32[8,128]{1,0:T(8,128)S(1)}, f32[8,128]{1,0:T(8,128)S(1)}, u32[]{:S(2)}, u32[]{:S(2)}) %collective-permute-start.19) | collective-permute-done | bytes 4128 | tf_op jit(solution)/shard_map/ppermute | solution.py:524
  144.1 0.9 collective-permute-start.20
  145.0 2.7 %collective-permute-done.20 = f32[8,128]{1,0:T(8,128)S(1)} collective-permute-done((f32[8,128]{1,0:T(8,128)S(1)}, f32[8,128]{1,0:T(8,128)S(1)}, u32[]{:S(2)}, u32[]{:S(2)}) %collective-permute-start.20) | collective-permute-done | bytes 4128 | tf_op jit(solution)/shard_map/ppermute | solution.py:523
  147.7 1.9 %collective-permute-start.21 = (f32[8,128]{1,0:T(8,128)S(1)}, f32[8,128]{1,0:T(8,128)S(1)}, u32[]{:S(2)}, u32[]{:S(2)}) collective-permute-start(f32[8,128]{1,0:T(8,128)S(1)} %add.62), channel_id=1, source_target_pairs={{32,64},{64,32},{96,0},{0,96},{33,65},{65,33},{97,1},{1,97},{34,66... | collective-permute-start | bytes 12296 | tf_op jit(solution)/shard_map/ppermute | solution.py:524
  149.6 2.9 %collective-permute-done.21 = f32[8,128]{1,0:T(8,128)S(1)} collective-permute-done((f32[8,128]{1,0:T(8,128)S(1)}, f32[8,128]{1,0:T(8,128)S(1)}, u32[]{:S(2)}, u32[]{:S(2)}) %collective-permute-start.21) | collective-permute-done | bytes 4128 | tf_op jit(solution)/shard_map/ppermute | solution.py:524
  152.6 3.0 %finish.1 = (f32[512,512]{1,0:T(8,128)}, f32[512,512]{1,0:T(8,128)}) custom-call(s32[2]{0:T(128)S(1)} %pad_add_fusion.1.place, f32[8,128]{1,0:T(8,128)S(1)} %add.56.sums_in.sums_one, f32[8,128]{1,0:T(8,128)S(1)} %add.63.sums_two, f32[544,640]{1,0:T(8,128)S(1)} %get-tuple-element.47.own_in, f32[32,640]{1,0:T(8,128)S(1)} %collective-permute-done.22.first_in.rim_l, ...), custom_call_target="tpu_custom_call" | custom-call | tf_op jit(solution)/shard_map/finish/pallas_call | solution.py:480
  (35 shorter events, 1.1 us)
Async XLA Ops:
  1.4 1.0 copy-start
  2.4 0.9 copy-start.1
  5.7 29.0 %all-to-all-start = ((bf16[16,2,160,128]{3,2,1,0:T(8,128)(2,1)}), bf16[16,2,160,128]{3,2,1,0:T(8,128)(2,1)S(1)}, u32[]{:S(2)}, u32[]{:S(2)}) async-start(bf16[16,2,160,128]{3,2,1,0:T(8,128)(2,1)} %bitcast.6), calls=%async_computation | async-start | bytes 2621440 | tf_op jit(solution)/shard_map/all_to_all | solution.py:552
  42.2 4.5 %collective-permute-start = (f32[32,640]{1,0:T(8,128)S(1)}, f32[32,640]{1,0:T(8,128)S(1)}, u32[]{:S(2)}, u32[]{:S(2)}) collective-permute-start(f32[32,640]{1,0:T(8,128)S(1)} %get-tuple-element.30), channel_id=1, source_target_pairs={{0,1},{1,0},{2,3},{3,2},{4,5},{5,4},{6,7},{7,6},{8,9},{9,8},{10,11... | collective-permute-start | bytes 245768 | tf_op jit(solution)/shard_map/ppermute | solution.py:519
  42.3 7.8 %collective-permute-start.1 = (f32[32,640]{1,0:T(8,128)S(1)}, f32[32,640]{1,0:T(8,128)S(1)}, u32[]{:S(2)}, u32[]{:S(2)}) collective-permute-start(f32[32,640]{1,0:T(8,128)S(1)} %get-tuple-element.31), channel_id=1, source_target_pairs={{1,2},{2,1},{3,4},{4,3},{5,6},{6,5},{7,8},{8,7},{9,10},{10,9},{11,... | collective-permute-start | bytes 245768 | tf_op jit(solution)/shard_map/ppermute | solution.py:519
  50.7 2.6 %collective-permute-start.2 = (f32[32,640]{1,0:T(8,128)S(1)}, f32[32,640]{1,0:T(8,128)S(1)}, u32[]{:S(2)}, u32[]{:S(2)}) collective-permute-start(f32[32,640]{1,0:T(8,128)S(1)} %get-tuple-element.34), channel_id=1, source_target_pairs={{0,16},{16,0},{32,48},{48,32},{64,80},{80,64},{96,112},{112,96},{1... | collective-permute-start | bytes 245768 | tf_op jit(solution)/shard_map/ppermute | solution.py:519
  50.8 5.2 %collective-permute-start.3 = (f32[32,640]{1,0:T(8,128)S(1)}, f32[32,640]{1,0:T(8,128)S(1)}, u32[]{:S(2)}, u32[]{:S(2)}) collective-permute-start(f32[32,640]{1,0:T(8,128)S(1)} %get-tuple-element.35), channel_id=1, source_target_pairs={{16,32},{32,16},{48,64},{64,48},{80,96},{96,80},{0,112},{112,0},{1... | collective-permute-start | bytes 245768 | tf_op jit(solution)/shard_map/ppermute | solution.py:519
  66.0 12.7 %collective-permute-start.11 = (f32[32,640]{1,0:T(8,128)S(1)}, f32[32,640]{1,0:T(8,128)S(1)}, u32[]{:S(2)}, u32[]{:S(2)}) collective-permute-start(f32[32,640]{1,0:T(8,128)S(1)} %get-tuple-element.39), channel_id=1, source_target_pairs={{0,1},{1,0},{2,3},{3,2},{4,5},{5,4},{6,7},{7,6},{8,9},{9,8},{10,11... | collective-permute-start | bytes 245768 | tf_op jit(solution)/shard_map/ppermute | solution.py:519
  66.0 12.7 %collective-permute-start.12 = (f32[32,640]{1,0:T(8,128)S(1)}, f32[32,640]{1,0:T(8,128)S(1)}, u32[]{:S(2)}, u32[]{:S(2)}) collective-permute-start(f32[32,640]{1,0:T(8,128)S(1)} %get-tuple-element.40), channel_id=1, source_target_pairs={{1,2},{2,1},{3,4},{4,3},{5,6},{6,5},{7,8},{8,7},{9,10},{10,9},{11,... | collective-permute-start | bytes 245768 | tf_op jit(solution)/shard_map/ppermute | solution.py:519
  67.6 3.6 %collective-permute-start.4 = (f32[8,128]{1,0:T(8,128)S(1)}, f32[8,128]{1,0:T(8,128)S(1)}, u32[]{:S(2)}, u32[]{:S(2)}) collective-permute-start(f32[8,128]{1,0:T(8,128)S(1)} %get-tuple-element.37), channel_id=1, source_target_pairs={{0,1},{1,0},{2,3},{3,2},{4,5},{5,4},{6,7},{7,6},{8,9},{9,8},{10,11... | collective-permute-start | bytes 12296 | tf_op jit(solution)/shard_map/ppermute | solution.py:523
  71.2 7.5 %collective-permute-start.5 = (f32[8,128]{1,0:T(8,128)S(1)}, f32[8,128]{1,0:T(8,128)S(1)}, u32[]{:S(2)}, u32[]{:S(2)}) collective-permute-start(f32[8,128]{1,0:T(8,128)S(1)} %add.50), channel_id=1, source_target_pairs={{1,2},{2,1},{3,0},{0,3},{5,6},{6,5},{7,4},{4,7},{9,10},{10,9},{11,... | collective-permute-start | bytes 12296 | tf_op jit(solution)/shard_map/ppermute | solution.py:524
  79.4 27.5 %collective-permute-start.13 = (f32[32,640]{1,0:T(8,128)S(1)}, f32[32,640]{1,0:T(8,128)S(1)}, u32[]{:S(2)}, u32[]{:S(2)}) collective-permute-start(f32[32,640]{1,0:T(8,128)S(1)} %get-tuple-element.43), channel_id=1, source_target_pairs={{0,16},{16,0},{32,48},{48,32},{64,80},{80,64},{96,112},{112,96},{1... | collective-permute-start | bytes 245768 | tf_op jit(solution)/shard_map/ppermute | solution.py:519
  79.4 27.4 %collective-permute-start.14 = (f32[32,640]{1,0:T(8,128)S(1)}, f32[32,640]{1,0:T(8,128)S(1)}, u32[]{:S(2)}, u32[]{:S(2)}) collective-permute-start(f32[32,640]{1,0:T(8,128)S(1)} %get-tuple-element.44), channel_id=1, source_target_pairs={{16,32},{32,16},{48,64},{64,48},{80,96},{96,80},{0,112},{112,0},{1... | collective-permute-start | bytes 245768 | tf_op jit(solution)/shard_map/ppermute | solution.py:519
  82.7 1.2 collective-permute-start.6
  83.9 8.3 %collective-permute-start.7 = (f32[8,128]{1,0:T(8,128)S(1)}, f32[8,128]{1,0:T(8,128)S(1)}, u32[]{:S(2)}, u32[]{:S(2)}) collective-permute-start(f32[8,128]{1,0:T(8,128)S(1)} %add.52), channel_id=1, source_target_pairs={{0,4},{4,0},{8,12},{12,8},{1,5},{5,1},{9,13},{13,9},{2,6},{6,2},{1... | collective-permute-start | bytes 12296 | tf_op jit(solution)/shard_map/ppermute | solution.py:523
  92.2 6.2 %collective-permute-start.8 = (f32[8,128]{1,0:T(8,128)S(1)}, f32[8,128]{1,0:T(8,128)S(1)}, u32[]{:S(2)}, u32[]{:S(2)}) collective-permute-start(f32[8,128]{1,0:T(8,128)S(1)} %add.53), channel_id=1, source_target_pairs={{4,8},{8,4},{12,0},{0,12},{5,9},{9,5},{13,1},{1,13},{6,10},{10,6},... | collective-permute-start | bytes 12296 | tf_op jit(solution)/shard_map/ppermute | solution.py:524
  98.4 3.6 %collective-permute-start.9 = (f32[8,128]{1,0:T(8,128)S(1)}, f32[8,128]{1,0:T(8,128)S(1)}, u32[]{:S(2)}, u32[]{:S(2)}) collective-permute-start(f32[8,128]{1,0:T(8,128)S(1)} %add.54), channel_id=1, source_target_pairs={{0,32},{32,0},{64,96},{96,64},{1,33},{33,1},{65,97},{97,65},{2,34}... | collective-permute-start | bytes 12296 | tf_op jit(solution)/shard_map/ppermute | solution.py:523
  102.0 4.8 %collective-permute-start.10 = (f32[8,128]{1,0:T(8,128)S(1)}, f32[8,128]{1,0:T(8,128)S(1)}, u32[]{:S(2)}, u32[]{:S(2)}) collective-permute-start(f32[8,128]{1,0:T(8,128)S(1)} %add.55), channel_id=1, source_target_pairs={{32,64},{64,32},{96,0},{0,96},{33,65},{65,33},{97,1},{1,97},{34,66... | collective-permute-start | bytes 12296 | tf_op jit(solution)/shard_map/ppermute | solution.py:524
  117.5 10.4 %collective-permute-start.22 = (f32[32,640]{1,0:T(8,128)S(1)}, f32[32,640]{1,0:T(8,128)S(1)}, u32[]{:S(2)}, u32[]{:S(2)}) collective-permute-start(f32[32,640]{1,0:T(8,128)S(1)} %get-tuple-element.48), channel_id=1, source_target_pairs={{0,1},{1,0},{2,3},{3,2},{4,5},{5,4},{6,7},{7,6},{8,9},{9,8},{10,11... | collective-permute-start | bytes 245768 | tf_op jit(solution)/shard_map/ppermute | solution.py:519
  117.6 10.3 %collective-permute-start.23 = (f32[32,640]{1,0:T(8,128)S(1)}, f32[32,640]{1,0:T(8,128)S(1)}, u32[]{:S(2)}, u32[]{:S(2)}) collective-permute-start(f32[32,640]{1,0:T(8,128)S(1)} %get-tuple-element.49), channel_id=1, source_target_pairs={{1,2},{2,1},{3,4},{4,3},{5,6},{6,5},{7,8},{8,7},{9,10},{10,9},{11,... | collective-permute-start | bytes 245768 | tf_op jit(solution)/shard_map/ppermute | solution.py:519
  119.5 3.6 %collective-permute-start.15 = (f32[8,128]{1,0:T(8,128)S(1)}, f32[8,128]{1,0:T(8,128)S(1)}, u32[]{:S(2)}, u32[]{:S(2)}) collective-permute-start(f32[8,128]{1,0:T(8,128)S(1)} %get-tuple-element.46), channel_id=1, source_target_pairs={{0,1},{1,0},{2,3},{3,2},{4,5},{5,4},{6,7},{7,6},{8,9},{9,8},{10,11... | collective-permute-start | bytes 12296 | tf_op jit(solution)/shard_map/ppermute | solution.py:523
  123.1 4.8 %collective-permute-start.16 = (f32[8,128]{1,0:T(8,128)S(1)}, f32[8,128]{1,0:T(8,128)S(1)}, u32[]{:S(2)}, u32[]{:S(2)}) collective-permute-start(f32[8,128]{1,0:T(8,128)S(1)} %add.57), channel_id=1, source_target_pairs={{1,2},{2,1},{3,0},{0,3},{5,6},{6,5},{7,4},{4,7},{9,10},{10,9},{11,... | collective-permute-start | bytes 12296 | tf_op jit(solution)/shard_map/ppermute | solution.py:524
  128.6 24.0 %collective-permute-start.24 = (f32[32,640]{1,0:T(8,128)S(1)}, f32[32,640]{1,0:T(8,128)S(1)}, u32[]{:S(2)}, u32[]{:S(2)}) collective-permute-start(f32[32,640]{1,0:T(8,128)S(1)} %get-tuple-element.52), channel_id=1, source_target_pairs={{0,16},{16,0},{32,48},{48,32},{64,80},{80,64},{96,112},{112,96},{1... | collective-permute-start | bytes 245768 | tf_op jit(solution)/shard_map/ppermute | solution.py:519
  128.7 23.9 %collective-permute-start.25 = (f32[32,640]{1,0:T(8,128)S(1)}, f32[32,640]{1,0:T(8,128)S(1)}, u32[]{:S(2)}, u32[]{:S(2)}) collective-permute-start(f32[32,640]{1,0:T(8,128)S(1)} %get-tuple-element.53), channel_id=1, source_target_pairs={{16,32},{32,16},{48,64},{64,48},{80,96},{96,80},{0,112},{112,0},{1... | collective-permute-start | bytes 245768 | tf_op jit(solution)/shard_map/ppermute | solution.py:519
  131.9 1.2 collective-permute-start.17
  133.0 4.9 %collective-permute-start.18 = (f32[8,128]{1,0:T(8,128)S(1)}, f32[8,128]{1,0:T(8,128)S(1)}, u32[]{:S(2)}, u32[]{:S(2)}) collective-permute-start(f32[8,128]{1,0:T(8,128)S(1)} %add.59), channel_id=1, source_target_pairs={{0,4},{4,0},{8,12},{12,8},{1,5},{5,1},{9,13},{13,9},{2,6},{6,2},{1... | collective-permute-start | bytes 12296 | tf_op jit(solution)/shard_map/ppermute | solution.py:523
  137.9 6.2 %collective-permute-start.19 = (f32[8,128]{1,0:T(8,128)S(1)}, f32[8,128]{1,0:T(8,128)S(1)}, u32[]{:S(2)}, u32[]{:S(2)}) collective-permute-start(f32[8,128]{1,0:T(8,128)S(1)} %add.60), channel_id=1, source_target_pairs={{4,8},{8,4},{12,0},{0,12},{5,9},{9,5},{13,1},{1,13},{6,10},{10,6},... | collective-permute-start | bytes 12296 | tf_op jit(solution)/shard_map/ppermute | solution.py:524
  144.1 3.6 %collective-permute-start.20 = (f32[8,128]{1,0:T(8,128)S(1)}, f32[8,128]{1,0:T(8,128)S(1)}, u32[]{:S(2)}, u32[]{:S(2)}) collective-permute-start(f32[8,128]{1,0:T(8,128)S(1)} %add.61), channel_id=1, source_target_pairs={{0,32},{32,0},{64,96},{96,64},{1,33},{33,1},{65,97},{97,65},{2,34}... | collective-permute-start | bytes 12296 | tf_op jit(solution)/shard_map/ppermute | solution.py:523
  147.7 4.8 %collective-permute-start.21 = (f32[8,128]{1,0:T(8,128)S(1)}, f32[8,128]{1,0:T(8,128)S(1)}, u32[]{:S(2)}, u32[]{:S(2)}) collective-permute-start(f32[8,128]{1,0:T(8,128)S(1)} %add.62), channel_id=1, source_target_pairs={{32,64},{64,32},{96,0},{0,96},{33,65},{65,33},{97,1},{1,97},{34,66... | collective-permute-start | bytes 12296 | tf_op jit(solution)/shard_map/ppermute | solution.py:524
where the time goes:
time: 156 us
  waiting for transfers between devices  60.2 us (39%)
  starting transfers between devices  56.3 us (36%)
  Pallas kernels  34.8 us (22%)
  local copies, waits for them, and re-layouts  1.94 us (1%)
    pallas_call x7, Pallas kernels, call(): pl.pallas_call(kernel, out_shape=[jax.ShapeDtypeStruct(shape, kind) for s...  32.4 us
    ppermute x6, starting transfers between devices, sum_pairs(): return value + lax.ppermute(value, axis, [(1, 2), (2, 1), (3, 0), (0, 3)])  20.7 us
    all_to_all x1, waiting for transfers between devices, body(): lax.all_to_all(sent.reshape(N_TX, CAP, SLOT_ROWS, 128), TX, split_axis=0,...  20.7 us
    ppermute x6, waiting for transfers between devices, sum_pairs(): value = value + lax.ppermute(value, axis, [(0, 1), (1, 0), (2, 3), (3, 2)])  15.2 us
    ppermute x12, starting transfers between devices, trade(): return (lax.ppermute(first, axes, near), lax.ppermute(second, axes, far))  15 us
    ppermute x6, waiting for transfers between devices, sum_pairs(): return value + lax.ppermute(value, axis, [(1, 2), (2, 1), (3, 0), (0, 3)])  13.6 us
    ppermute x6, starting transfers between devices, sum_pairs(): value = value + lax.ppermute(value, axis, [(0, 1), (1, 0), (2, 3), (3, 2)])  12.5 us
    ppermute x12, waiting for transfers between devices, trade(): return (lax.ppermute(first, axes, near), lax.ppermute(second, axes, far))  8.38 us
  transfers between devices with their start and end apart: 27, of which 18 were waited for; matrix products, arithmetic and copies ran while one was open for 0% of the time, Pallas kernels for 0%

commit v1 on v0

--- a/solution.py
+++ b/solution.py
@@ -22,9 +22,9 @@
 RIM = 2 * HALO
 WIN = BLOCK + 2 * HALO
 SLOT_ROWS = 160
-GROUP = 4
+GROUP = 8
 F32, BF16 = jnp.float32, jnp.bfloat16
-VMEM_BYTES = 38 << 20
+VMEM_BYTES = 36 << 20
 
 
 def iota(shape, axis):
@@ -37,50 +37,60 @@
     return jnp.where(lane < 64, low, high)
 
 
-def pack_kernel(labels, spread_ref, exposures_ref, out_ref, pad, kern):
+def pack_kernel(labels, spread_hbm, exposures_hbm, out_ref, points, images, pad, kern, sems):
+    copies = [
+        pltpu.make_async_copy(spread_hbm, points, sems.at[0]),
+        pltpu.make_async_copy(exposures_hbm, images, sems.at[1]),
+    ]
+    for copy in copies:
+        copy.start()
+    for s in range(SLOTS):
+        out_ref[s, 128:SLOT_ROWS, :] = jnp.zeros((SLOT_ROWS - 128, 128), BF16)
     pad[...] = jnp.zeros_like(pad)
+    frame = iota((FB, 128), 0)
+    row_frac, col_frac = jnp.zeros((FB, 128), F32), jnp.zeros((FB, 128), F32)
     for f in range(FB):
-        pad[f, 0:PSF, 0:PSF] = spread_ref[:, f, :]
-    for f in range(FB):
-        point = pad[f]
-        point = point / jnp.sum(point, keepdims=True)
-        row_frac = labels[0, f].astype(F32) / SUB
-        col_frac = labels[1, f].astype(F32) / SUB
+        row_frac = jnp.where(frame == f, labels[0, f].astype(F32) / SUB, row_frac)
+        col_frac = jnp.where(frame == f, labels[1, f].astype(F32) / SUB, col_frac)
+    copies[0].wait()
+    pad[0:PSF, :, 0:PSF] = points[...]
+    total = jnp.sum(jnp.sum(pad[...], axis=0), axis=1, keepdims=True)
+    before = jnp.zeros((FB, 128), F32)
+    for a in range(TAPS):
+        point = pad[a] / total
         blended = (1.0 - col_frac) * point + col_frac * pltpu.roll(point, 1, 1)
-        lowered = pltpu.roll(blended, 1, 0)
-        kern[32 * f : 32 * f + 32, :] = (
-            (1.0 - row_frac) * blended + row_frac * lowered
-        ).astype(BF16)
+        kern[FB * a : FB * a + FB, :] = (1.0 - row_frac) * blended + row_frac * before
+        before = blended
+    taps = kern[...].astype(BF16)
     row, lane = iota((128, 128), 0), iota((128, 128), 1)
     tall, wide = iota((32 * FB, 128), 0), iota((32 * FB, 128), 1)
-    tap = tall & 31
+    tap = tall >> 3
     place = jnp.where((lane & 31) == 31 - row, 1.0, 0.0).astype(BF16)
-    spread = jnp.dot(kern[...], place, preferred_element_type=F32)
+    spread = jnp.dot(taps, place, preferred_element_type=F32)
     spread = jnp.where((wide >> 5) == ((tap >> 2) & 3), spread, 0.0).astype(BF16)
     target, source = iota((8 * FB, 32 * FB), 0), iota((8 * FB, 32 * FB), 1)
-    s_tap = source & 31
-    pick = ((source >> 5) == (target >> 3)) & (
+    s_tap = source >> 3
+    pick = ((source & 7) == (target >> 3)) & (
         (target & 7) == 2 * (s_tap & 3) + (s_tap >> 4)
     )
     backward = jnp.dot(
         jnp.where(pick, 1.0, 0.0).astype(BF16), spread, preferred_element_type=F32
     )
     place = jnp.where((lane & 63) == row, 1.0, 0.0).astype(BF16)
-    spread = jnp.dot(kern[...], place, preferred_element_type=F32)
+    spread = jnp.dot(taps, place, preferred_element_type=F32)
     spread = jnp.where((wide >> 6) == (tap & 1), spread, 0.0).astype(BF16)
     target, source = iota((16 * FB, 32 * FB), 0), iota((16 * FB, 32 * FB), 1)
-    pick = ((source >> 5) == (target >> 4)) & ((target & 15) == ((source & 31) >> 1))
+    pick = ((source & 7) == (target >> 4)) & ((target & 15) == (source >> 4))
     ahead = jnp.dot(
         jnp.where(pick, 1.0, 0.0).astype(BF16), spread, preferred_element_type=F32
     )
-    for s in range(SLOTS):
-        out_ref[s, 128:SLOT_ROWS, :] = jnp.zeros((SLOT_ROWS - 128, 128), BF16)
+    copies[1].wait()
     for f in range(FB):
         standing = jnp.int32(0)
         for g in range(f):
             standing = standing + jnp.where(labels[2, g] == labels[2, f], 1, 0)
         slot = CAP * labels[2, f] + jnp.minimum(standing, CAP - 1)
-        out_ref[slot, 0:BLOCK, :] = exposures_ref[f].astype(BF16)
+        out_ref[slot, 0:BLOCK, :] = images[f].astype(BF16)
         tail = jnp.concatenate(
             [
                 backward[8 * f : 8 * f + 8],
@@ -90,20 +100,6 @@
             axis=0,
         )
         out_ref[slot, 128:SLOT_ROWS, :] = tail.astype(BF16)
-
-
-def pack(labels, spread, exposures):
-    smem = pl.BlockSpec(memory_space=pltpu.SMEM)
-    vmem = pl.BlockSpec(memory_space=pltpu.VMEM)
-    return pl.pallas_call(
-        pack_kernel,
-        out_shape=jax.ShapeDtypeStruct((SLOTS, SLOT_ROWS, 128), BF16),
-        in_specs=[smem, vmem, vmem],
-        out_specs=vmem,
-        scratch_shapes=[pltpu.VMEM((FB, 32, 128), F32), pltpu.VMEM((32 * FB, 128), BF16)],
-        compiler_params=pltpu.CompilerParams(vmem_limit_bytes=VMEM_BYTES),
-        name="pack",
-    )(labels, spread, exposures)
 
 
 def list_frames(cells, frames):
@@ -301,8 +297,8 @@
 
 
 def first_kernel(
-    cells, place, slots_ref, own_ref, left_ref, right_ref, top_ref, bottom_ref, taps_out,
-    frames, taps, total, turned, spread, sems,
+    cells, place, slots_ref, own_ref, left_ref, right_ref, top_ref, bottom_ref, taps,
+    frames, total, turned, spread,
 ):
     count = list_frames(cells, frames)
     clear_total(total)
@@ -311,7 +307,6 @@
     def step(group, carry):
         for i in group:
             build_taps(slots_ref[frames[i], 128:SLOT_ROWS].astype(F32), taps.at[i])
-            pltpu.make_async_copy(taps.at[i], taps_out.at[i], sems.at[i]).start()
         for g, i in enumerate(group):
             image = slots_ref[frames[i], 0:BLOCK].astype(F32)
             expand(image, turned.at[g], spread.at[g])
@@ -323,22 +318,14 @@
     fold(total, own_ref)
     write_rims(place, own_ref, left_ref, right_ref, top_ref, bottom_ref)
 
-    def wait(i, carry):
-        pltpu.make_async_copy(taps.at[i], taps_out.at[i], sems.at[i]).wait()
-        return carry
-
-    lax.fori_loop(0, count, wait, 0)
-
-
-def frame_pass(cells, frames, count, taps_in, field, scratch):
-    taps, total, turned, spread, stack, copies, doubled, product, paired, sems = scratch
+
+def frame_pass(cells, frames, count, taps, field, scratch):
+    total, turned, spread, stack, copies, doubled, product, paired = scratch
     unfold(field, copies, doubled, stack)
     clear_total(total)
     clear_margins(turned, spread)
 
     def step(group, sums):
-        for i in group:
-            pltpu.make_async_copy(taps_in.at[i], taps.at[i], sems.at[i]).wait()
         for g, i in enumerate(group):
             lx, top = place_of(cells, frames, i)
             window = stack[pl.ds(lx, 4), pl.ds(pl.multiple_of(top, 128), WIN), :]
@@ -368,28 +355,17 @@
     return over_frames(count, step, jnp.zeros((1, 128), F32))
 
 
-def start_taps(cells, frames, taps_in, taps, sems):
-    count = list_frames(cells, frames)
-
-    def start(i, carry):
-        pltpu.make_async_copy(taps_in.at[i], taps.at[i], sems.at[i]).start()
-        return carry
-
-    lax.fori_loop(0, count, start, 0)
-    return count
-
-
 def second_kernel(
-    cells, place, own_in, rim_l, rim_r, rim_a, rim_b, taps_in,
+    cells, place, own_in, rim_l, rim_r, rim_a, rim_b, taps,
     own_ref, left_ref, right_ref, top_ref, bottom_ref, residual_ref, sums_ref,
     frames, field, *scratch,
 ):
-    count = start_taps(cells, frames, taps_in, scratch[0], scratch[-1])
+    count = list_frames(cells, frames)
     complete(place, own_in, (rim_l, rim_r, rim_a, rim_b), field)
     residual_ref[...] = field[0:EXT, :]
     square = inner_sum(lambda r, n: field[r : r + n, :] * field[r : r + n, :])
-    curve = frame_pass(cells, frames, count, taps_in, field, scratch)
-    fold(scratch[1], own_ref)
+    curve = frame_pass(cells, frames, count, taps, field, scratch)
+    fold(scratch[0], own_ref)
     write_rims(place, own_ref, left_ref, right_ref, top_ref, bottom_ref)
     sums_ref[...] = jnp.zeros_like(sums_ref)
     sums_ref[0:1] = square
@@ -403,11 +379,11 @@
 
 
 def third_kernel(
-    cells, place, sums_in, own_in, rim_l, rim_r, rim_a, rim_b, start_ref, taps_in,
+    cells, place, sums_in, own_in, rim_l, rim_r, rim_a, rim_b, start_ref, taps,
     own_ref, left_ref, right_ref, top_ref, bottom_ref, residual_ref, applied_ref, sums_ref,
     frames, field, *scratch,
 ):
-    count = start_taps(cells, frames, taps_in, scratch[0], scratch[-1])
+    count = list_frames(cells, frames)
     complete(place, own_in, (rim_l, rim_r, rim_a, rim_b), field)
     step = first_step(sums_in[...])[2]
     for r in range(0, EXT, 32):
@@ -419,8 +395,8 @@
         field[r : r + 32, :] = residual
     square = inner_sum(lambda r, n: field[r : r + n, :] * field[r : r + n, :])
     cross = inner_sum(lambda r, n: field[r : r + n, :] * applied_ref[r : r + n, :])
-    curve = frame_pass(cells, frames, count, taps_in, field, scratch)
-    fold(scratch[1], own_ref)
+    curve = frame_pass(cells, frames, count, taps, field, scratch)
+    fold(scratch[0], own_ref)
     write_rims(place, own_ref, left_ref, right_ref, top_ref, bottom_ref)
     sums_ref[...] = jnp.zeros_like(sums_ref)
     sums_ref[0:1] = square
@@ -471,19 +447,20 @@
     second_out[...] = jnp.where(even, top[...], bottom[...])
 
 
-def call(kernel, outs, spaces, operands, scratch, name, out_spaces=None):
+def call(kernel, outs, spaces, operands, scratch, name, vmem=VMEM_BYTES):
     specs = {
         "s": pl.BlockSpec(memory_space=pltpu.SMEM),
         "v": pl.BlockSpec(memory_space=pltpu.VMEM),
         "a": pl.BlockSpec(memory_space=pl.ANY),
+        "h": pl.BlockSpec(memory_space=pltpu.HBM),
     }
     return pl.pallas_call(
         kernel,
         out_shape=[jax.ShapeDtypeStruct(shape, kind) for shape, kind in outs],
         in_specs=[specs[space] for space in spaces],
-        out_specs=[specs[space] for space in (out_spaces or "v" * len(outs))],
+        out_specs=[specs["v"]] * len(outs),
         scratch_shapes=scratch,
-        compiler_params=pltpu.CompilerParams(vmem_limit_bytes=VMEM_BYTES),
+        compiler_params=pltpu.CompilerParams(vmem_limit_bytes=vmem),
         name=name,
     )(*operands)
 
@@ -492,7 +469,7 @@
 RIM_ARRAY = ((RIM, LANES), F32)
 SUMS = ((8, 128), F32)
 FRAME_LIST = pltpu.SMEM((SLOTS + 1,), jnp.int32)
-TAPS_SCRATCH = pltpu.VMEM((SLOTS, 2, 256, 256), BF16)
+ALL_TAPS = ((SLOTS, 2, 256, 256), BF16)
 TOTAL = pltpu.VMEM((TILE // 32 + 1, 8 + EXT, 256), F32)
 TURNED = pltpu.VMEM((GROUP, 4, WIN, 128), F32)
 SPREAD = pltpu.VMEM((GROUP, 4, WIN + 16, 128), BF16)
@@ -500,7 +477,6 @@
 PASS_SCRATCH = [
     FRAME_LIST,
     FIELD_SCRATCH,
-    TAPS_SCRATCH,
     TOTAL,
     TURNED,
     SPREAD,
@@ -509,7 +485,6 @@
     pltpu.VMEM((4, EXT + 8, 128), F32),
     pltpu.VMEM((GROUP, 4, WIN, 256), F32),
     pltpu.VMEM((GROUP, 4, 144, 128), F32),
-    pltpu.SemaphoreType.DMA((SLOTS,)),
 ]
 
 
@@ -548,7 +523,21 @@
 def body(exposures, point_spread, warp_steps, column, block_cell):
     place = jnp.stack([lax.axis_index(TY), lax.axis_index(TX)]).astype(jnp.int32)
     labels = jnp.concatenate([warp_steps.T, column.T, block_cell[None]])
-    sent = pack(labels, point_spread.transpose(1, 0, 2), exposures)
+    (sent,) = call(
+        pack_kernel,
+        [((SLOTS, SLOT_ROWS, 128), BF16)],
+        "shh",
+        (labels, point_spread.transpose(1, 0, 2), exposures),
+        [
+            pltpu.VMEM((PSF, FB, PSF), F32),
+            pltpu.VMEM((FB, BLOCK, BLOCK), F32),
+            pltpu.VMEM((TAPS, FB, 128), F32),
+            pltpu.VMEM((TAPS * FB, 128), F32),
+            pltpu.SemaphoreType.DMA((2,)),
+        ],
+        "pack",
+        60 << 20,
+    )
     slots = lax.all_to_all(
         sent.reshape(N_TX, CAP, SLOT_ROWS, 128), TX, split_axis=0, concat_axis=0, tiled=True
     ).reshape(SLOTS, SLOT_ROWS, 128)
@@ -557,18 +546,17 @@
 
     own, left, right, top, bottom, taps = call(
         first_kernel,
-        [FIELD] + rims_out + [((SLOTS, 2, 256, 256), BF16)],
+        [FIELD] + rims_out + [ALL_TAPS],
         "ssv",
         (cells, place, slots),
-        [FRAME_LIST, TAPS_SCRATCH, TOTAL, TURNED, SPREAD, pltpu.SemaphoreType.DMA((SLOTS,))],
+        [FRAME_LIST, TOTAL, TURNED, SPREAD],
         "right_side",
-        "vvvvva",
     )
     rims, _ = trade_rims(place, left, right, top, bottom)
     own, left, right, top, bottom, start, sums_one = call(
         second_kernel,
         [FIELD] + rims_out + [FIELD, SUMS],
-        "ssvvvvva",
+        "ssvvvvvv",
         (cells, place, own, *rims, taps),
         PASS_SCRATCH,
         "first_pass",
@@ -577,7 +565,7 @@
     own, left, right, top, bottom, residual, applied, sums_two = call(
         third_kernel,
         [FIELD] + rims_out + [FIELD, FIELD, SUMS],
-        "ssvvvvvvva",
+        "ssvvvvvvvv",
         (cells, place, sums_one, own, *rims, start, taps),
         PASS_SCRATCH,
         "second_pass",

time: 156 us -> 150 us (0.962); the launches traced: 156 us -> 147 us
  starting transfers between devices: 56.3 us -> 39.6 us
  waiting for transfers between devices: 60.2 us -> 66.6 us
  Pallas kernels: 34.8 us -> 37.7 us
  local copies, waits for them, and re-layouts: 1.94 us -> 0 us
    ppermute x6, starting transfers between devices: 20.7 us -> 7.55 us  [sum_pairs(): return value + lax.ppermute(value, axis, [(1, 2), (2, 1), (3, 0), (0, 3)])]
    ppermute x12, starting transfers between devices: 15 us -> 5.83 us  [trade(): return (lax.ppermute(first, axes, near), lax.ppermute(second, axes, far))]
    ppermute x6, waiting for transfers between devices: 13.6 us -> 21.4 us  [sum_pairs(): return value + lax.ppermute(value, axis, [(1, 2), (2, 1), (3, 0), (0, 3)])]
    ppermute x6, starting transfers between devices: 12.5 us -> 18.1 us  [sum_pairs(): value = value + lax.ppermute(value, axis, [(0, 1), (1, 0), (2, 3), (3, 2)])]
    pallas_call x7 -> x8, Pallas kernels: 32.4 us -> 37.7 us  [call(): pl.pallas_call(kernel, out_shape=[jax.ShapeDtypeStruct(shape, kind) for s...]
    ppermute x6, waiting for transfers between devices: 15.2 us -> 12.2 us  [sum_pairs(): value = value + lax.ppermute(value, axis, [(0, 1), (1, 0), (2, 3), (3, 2)])]
    pallas_call x1 -> x0, Pallas kernels: 2.4 us -> none  [pack(): pl.pallas_call(pack_kernel, out_shape=jax.ShapeDtypeStruct((SLOTS, SLOT_R...]
    unnamed x4 -> x0, local copies, waits for them, and re-layouts: 1.94 us -> none
where the time goes in v1:
time: 150 us; the launch traced here: 147 us
  waiting for transfers between devices  66.6 us (44%)
  starting transfers between devices  39.6 us (26%)
  Pallas kernels  37.7 us (25%)
  other arithmetic  2.08 us (1%)
    pallas_call x8, Pallas kernels, call(): pl.pallas_call(kernel, out_shape=[jax.ShapeDtypeStruct(shape, kind) for s...  37.7 us
    ppermute x6, waiting for transfers between devices, sum_pairs(): return value + lax.ppermute(value, axis, [(1, 2), (2, 1), (3, 0), (0, 3)])  21.4 us
    all_to_all x1, waiting for transfers between devices, body(): lax.all_to_all(sent.reshape(N_TX, CAP, SLOT_ROWS, 128), TX, split_axis=0,...  20.7 us
    ppermute x6, starting transfers between devices, sum_pairs(): value = value + lax.ppermute(value, axis, [(0, 1), (1, 0), (2, 3), (3, 2)])  18.1 us
    ppermute x6, waiting for transfers between devices, sum_pairs(): value = value + lax.ppermute(value, axis, [(0, 1), (1, 0), (2, 3), (3, 2)])  12.2 us
    ppermute x12, waiting for transfers between devices, trade(): return (lax.ppermute(first, axes, near), lax.ppermute(second, axes, far))  9.98 us
    all_to_all x1, starting transfers between devices, body(): lax.all_to_all(sent.reshape(N_TX, CAP, SLOT_ROWS, 128), TX, split_axis=0,...  8.14 us
    ppermute x6, starting transfers between devices, sum_pairs(): return value + lax.ppermute(value, axis, [(1, 2), (2, 1), (3, 0), (0, 3)])  7.55 us
  transfers between devices with their start and end apart: 27, of which 18 were waited for; matrix products, arithmetic and copies ran while one was open for 0% of the time, Pallas kernels for 0%

profile of v1, /device:TPU:0, one launch (start us, length us, event | category | flops | bytes accessed | tf_op | source)
XLA Modules:
  0.0 146.7 jit_solution(982736973393786464)
XLA Ops:
  0.6 1.3 pad_add_fusion.labels
  1.9 3.4 %pack.1 = bf16[32,160,128]{2,1,0:T(8,128)(2,1)} custom-call(s32[4,8]{1,0:T(4,128)} %pad_add_fusion.labels, f32[31,8,31]{2,1,0:T(8,128)} %bitcast.11, f32[8,128,128]{2,1,0:T(8,128)} %exposures_hbm.1), custom_call_target="tpu_custom_call" | custom-call | tf_op jit(solution)/shard_map/pack/pallas_call | solution.py:457
  5.3 8.1 %all-to-all-start = ((bf16[16,2,160,128]{3,2,1,0:T(8,128)(2,1)}), bf16[16,2,160,128]{3,2,1,0:T(8,128)(2,1)S(1)}, u32[]{:S(2)}, u32[]{:S(2)}) async-start(bf16[16,2,160,128]{3,2,1,0:T(8,128)(2,1)} %bitcast.10), calls=%async_computation | async-start | bytes 2621440 | tf_op jit(solution)/shard_map/all_to_all | solution.py:541
  13.6 20.7 %all-to-all-done = bf16[16,2,160,128]{3,2,1,0:T(8,128)(2,1)S(1)} async-done(((bf16[16,2,160,128]{3,2,1,0:T(8,128)(2,1)}), bf16[16,2,160,128]{3,2,1,0:T(8,128)(2,1)S(1)}, u32[]{:S(2)}, u32[]{:S(2)}) %all-to-all-start) | async-done | bytes 1310752 | tf_op jit(solution)/shard_map/all_to_all | solution.py:541
  34.3 0.7 fusion.cells
  35.0 6.3 %right_side.1 = (f32[544,640]{1,0:T(8,128)S(1)}, f32[32,640]{1,0:T(8,128)S(1)}, f32[32,640]{1,0:T(8,128)S(1)}, f32[32,640]{1,0:T(8,128)S(1)}, f32[32,640]{1,0:T(...) custom-call(s32[32]{0:T(128)S(1)} %fusion.cells, s32[2]{0:T(128)S(1)} %pad_add_fusion.1.place, bf16[32,160,128]{2,1,0:T(8,128)(2,1)S(1)} %bitcast.9), custom_call_target="tpu_custom_call" | custom-call | tf_op jit(solution)/shard_map/right_side/pallas_call | solution.py:457
  41.3 0.1 collective-permute-start
  41.4 0.9 collective-permute-start.1
  42.3 3.5 %collective-permute-done.first_in.rim_l = f32[32,640]{1,0:T(8,128)S(1)} collective-permute-done((f32[32,640]{1,0:T(8,128)S(1)}, f32[32,640]{1,0:T(8,128)S(1)}, u32[]{:S(2)}, u32[]{:S(2)}) %collective-permute-start) | collective-permute-done | bytes 81952 | tf_op jit(solution)/shard_map/ppermute | solution.py:494
  45.8 3.4 %collective-permute-done.1.second_in.rim_r = f32[32,640]{1,0:T(8,128)S(1)} collective-permute-done((f32[32,640]{1,0:T(8,128)S(1)}, f32[32,640]{1,0:T(8,128)S(1)}, u32[]{:S(2)}, u32[]{:S(2)}) %collective-permute-start.1) | collective-permute-done | bytes 81952 | tf_op jit(solution)/shard_map/ppermute | solution.py:494
  49.2 0.6 corners.3
  49.9 2.1 %collective-permute-start.3 = (f32[32,640]{1,0:T(8,128)S(1)}, f32[32,640]{1,0:T(8,128)S(1)}, u32[]{:S(2)}, u32[]{:S(2)}) collective-permute-start(f32[32,640]{1,0:T(8,128)S(1)} %get-tuple-element.35), channel_id=1, source_target_pairs={{16,32},{32,16},{48,64},{64,48},{80,96},{96,80},{0,112},{112,0},{1... | collective-permute-start | bytes 245768 | tf_op jit(solution)/shard_map/ppermute | solution.py:494
  52.1 3.0 %collective-permute-done.3.rim_b = f32[32,640]{1,0:T(8,128)S(1)} collective-permute-done((f32[32,640]{1,0:T(8,128)S(1)}, f32[32,640]{1,0:T(8,128)S(1)}, u32[]{:S(2)}, u32[]{:S(2)}) %collective-permute-start.3) | collective-permute-done | bytes 81952 | tf_op jit(solution)/shard_map/ppermute | solution.py:494
  55.1 11.2 %first_pass.1 = (f32[544,640]{1,0:T(8,128)S(1)}, f32[32,640]{1,0:T(8,128)S(1)}, f32[32,640]{1,0:T(8,128)S(1)}, f32[32,640]{1,0:T(8,128)S(1)}, f32[32,640]{1,0:T(...) custom-call(s32[32]{0:T(128)S(1)} %fusion.cells, s32[2]{0:T(128)S(1)} %pad_add_fusion.1.place, ...), custom_call_target="tpu_custom_call" | custom-call | tf_op jit(solution)/shard_map/first_pass/pallas_call | solution.py:457
  66.3 0.1 collective-permute-start.11
  66.4 0.1 collective-permute-start.12
  66.5 5.7 %collective-permute-start.4 = (f32[8,128]{1,0:T(8,128)S(1)}, f32[8,128]{1,0:T(8,128)S(1)}, u32[]{:S(2)}, u32[]{:S(2)}) collective-permute-start(f32[8,128]{1,0:T(8,128)S(1)} %get-tuple-element.37), channel_id=1, source_target_pairs={{0,1},{1,0},{2,3},{3,2},{4,5},{5,4},{6,7},{7,6},{8,9},{9,8},{10,11... | collective-permute-start | bytes 12296 | tf_op jit(solution)/shard_map/ppermute | solution.py:498
  72.2 1.6 %collective-permute-done.4 = f32[8,128]{1,0:T(8,128)S(1)} collective-permute-done((f32[8,128]{1,0:T(8,128)S(1)}, f32[8,128]{1,0:T(8,128)S(1)}, u32[]{:S(2)}, u32[]{:S(2)}) %collective-permute-start.4) | collective-permute-done | bytes 4128 | tf_op jit(solution)/shard_map/ppermute | solution.py:498
  73.8 1.7 %collective-permute-start.5 = (f32[8,128]{1,0:T(8,128)S(1)}, f32[8,128]{1,0:T(8,128)S(1)}, u32[]{:S(2)}, u32[]{:S(2)}) collective-permute-start(f32[8,128]{1,0:T(8,128)S(1)} %add.50), channel_id=1, source_target_pairs={{1,2},{2,1},{3,0},{0,3},{5,6},{6,5},{7,4},{4,7},{9,10},{10,9},{11,... | collective-permute-start | bytes 12296 | tf_op jit(solution)/shard_map/ppermute | solution.py:499
  75.5 3.1 %collective-permute-done.5 = f32[8,128]{1,0:T(8,128)S(1)} collective-permute-done((f32[8,128]{1,0:T(8,128)S(1)}, f32[8,128]{1,0:T(8,128)S(1)}, u32[]{:S(2)}, u32[]{:S(2)}) %collective-permute-start.5) | collective-permute-done | bytes 4128 | tf_op jit(solution)/shard_map/ppermute | solution.py:499
  78.6 0.6 corners.4
  79.4 0.8 collective-permute-start.14
  80.2 1.2 collective-permute-done.6
  81.4 4.0 %collective-permute-start.7 = (f32[8,128]{1,0:T(8,128)S(1)}, f32[8,128]{1,0:T(8,128)S(1)}, u32[]{:S(2)}, u32[]{:S(2)}) collective-permute-start(f32[8,128]{1,0:T(8,128)S(1)} %add.52), channel_id=1, source_target_pairs={{0,4},{4,0},{8,12},{12,8},{1,5},{5,1},{9,13},{13,9},{2,6},{6,2},{1... | collective-permute-start | bytes 12296 | tf_op jit(solution)/shard_map/ppermute | solution.py:498
  85.4 1.6 %collective-permute-done.7 = f32[8,128]{1,0:T(8,128)S(1)} collective-permute-done((f32[8,128]{1,0:T(8,128)S(1)}, f32[8,128]{1,0:T(8,128)S(1)}, u32[]{:S(2)}, u32[]{:S(2)}) %collective-permute-start.7) | collective-permute-done | bytes 4128 | tf_op jit(solution)/shard_map/ppermute | solution.py:498
  87.0 4.8 %collective-permute-done.8 = f32[8,128]{1,0:T(8,128)S(1)} collective-permute-done((f32[8,128]{1,0:T(8,128)S(1)}, f32[8,128]{1,0:T(8,128)S(1)}, u32[]{:S(2)}, u32[]{:S(2)}) %collective-permute-start.8) | collective-permute-done | bytes 4128 | tf_op jit(solution)/shard_map/ppermute | solution.py:499
  91.8 0.5 collective-permute-start.9
  92.3 3.1 %collective-permute-done.9 = f32[8,128]{1,0:T(8,128)S(1)} collective-permute-done((f32[8,128]{1,0:T(8,128)S(1)}, f32[8,128]{1,0:T(8,128)S(1)}, u32[]{:S(2)}, u32[]{:S(2)}) %collective-permute-start.9) | collective-permute-done | bytes 4128 | tf_op jit(solution)/shard_map/ppermute | solution.py:498
  95.4 1.4 collective-permute-start.10
  96.8 3.4 %collective-permute-done.10 = f32[8,128]{1,0:T(8,128)S(1)} collective-permute-done((f32[8,128]{1,0:T(8,128)S(1)}, f32[8,128]{1,0:T(8,128)S(1)}, u32[]{:S(2)}, u32[]{:S(2)}) %collective-permute-start.10) | collective-permute-done | bytes 4128 | tf_op jit(solution)/shard_map/ppermute | solution.py:499
  100.2 11.8 %second_pass.1 = (f32[544,640]{1,0:T(8,128)S(1)}, f32[32,640]{1,0:T(8,128)S(1)}, f32[32,640]{1,0:T(8,128)S(1)}, f32[32,640]{1,0:T(8,128)S(1)}, f32[32,640]{1,0:T...) custom-call(s32[32]{0:T(128)S(1)} %fusion.cells, s32[2]{0:T(128)S(1)} %pad_add_fusion.1.place, ...), custom_call_target="tpu_custom_call" | custom-call | tf_op jit(solution)/shard_map/second_pass/pallas_call | solution.py:457
  112.0 0.1 collective-permute-start.22
  112.1 0.1 collective-permute-start.23
  112.2 3.0 %collective-permute-start.15 = (f32[8,128]{1,0:T(8,128)S(1)}, f32[8,128]{1,0:T(8,128)S(1)}, u32[]{:S(2)}, u32[]{:S(2)}) collective-permute-start(f32[8,128]{1,0:T(8,128)S(1)} %get-tuple-element.46), channel_id=1, source_target_pairs={{0,1},{1,0},{2,3},{3,2},{4,5},{5,4},{6,7},{7,6},{8,9},{9,8},{10,11... | collective-permute-start | bytes 12296 | tf_op jit(solution)/shard_map/ppermute | solution.py:498
  115.2 1.6 %collective-permute-done.15 = f32[8,128]{1,0:T(8,128)S(1)} collective-permute-done((f32[8,128]{1,0:T(8,128)S(1)}, f32[8,128]{1,0:T(8,128)S(1)}, u32[]{:S(2)}, u32[]{:S(2)}) %collective-permute-start.15) | collective-permute-done | bytes 4128 | tf_op jit(solution)/shard_map/ppermute | solution.py:498
  116.8 2.5 %collective-permute-start.16 = (f32[8,128]{1,0:T(8,128)S(1)}, f32[8,128]{1,0:T(8,128)S(1)}, u32[]{:S(2)}, u32[]{:S(2)}) collective-permute-start(f32[8,128]{1,0:T(8,128)S(1)} %add.57), channel_id=1, source_target_pairs={{1,2},{2,1},{3,0},{0,3},{5,6},{6,5},{7,4},{4,7},{9,10},{10,9},{11,... | collective-permute-start | bytes 12296 | tf_op jit(solution)/shard_map/ppermute | solution.py:499
  119.4 2.3 %collective-permute-done.16 = f32[8,128]{1,0:T(8,128)S(1)} collective-permute-done((f32[8,128]{1,0:T(8,128)S(1)}, f32[8,128]{1,0:T(8,128)S(1)}, u32[]{:S(2)}, u32[]{:S(2)}) %collective-permute-start.16) | collective-permute-done | bytes 4128 | tf_op jit(solution)/shard_map/ppermute | solution.py:499
  121.7 0.6 corners.5
  122.4 1.3 collective-permute-start.25
  123.7 1.2 collective-permute-done.17
  124.8 4.0 %collective-permute-start.18 = (f32[8,128]{1,0:T(8,128)S(1)}, f32[8,128]{1,0:T(8,128)S(1)}, u32[]{:S(2)}, u32[]{:S(2)}) collective-permute-start(f32[8,128]{1,0:T(8,128)S(1)} %add.59), channel_id=1, source_target_pairs={{0,4},{4,0},{8,12},{12,8},{1,5},{5,1},{9,13},{13,9},{2,6},{6,2},{1... | collective-permute-start | bytes 12296 | tf_op jit(solution)/shard_map/ppermute | solution.py:498
  128.8 1.6 %collective-permute-done.18 = f32[8,128]{1,0:T(8,128)S(1)} collective-permute-done((f32[8,128]{1,0:T(8,128)S(1)}, f32[8,128]{1,0:T(8,128)S(1)}, u32[]{:S(2)}, u32[]{:S(2)}) %collective-permute-start.18) | collective-permute-done | bytes 4128 | tf_op jit(solution)/shard_map/ppermute | solution.py:498
  130.4 4.8 %collective-permute-done.19 = f32[8,128]{1,0:T(8,128)S(1)} collective-permute-done((f32[8,128]{1,0:T(8,128)S(1)}, f32[8,128]{1,0:T(8,128)S(1)}, u32[]{:S(2)}, u32[]{:S(2)}) %collective-permute-start.19) | collective-permute-done | bytes 4128 | tf_op jit(solution)/shard_map/ppermute | solution.py:499
  135.2 0.9 collective-permute-start.20
  136.1 2.7 %collective-permute-done.20 = f32[8,128]{1,0:T(8,128)S(1)} collective-permute-done((f32[8,128]{1,0:T(8,128)S(1)}, f32[8,128]{1,0:T(8,128)S(1)}, u32[]{:S(2)}, u32[]{:S(2)}) %collective-permute-start.20) | collective-permute-done | bytes 4128 | tf_op jit(solution)/shard_map/ppermute | solution.py:498
  138.8 1.8 %collective-permute-start.21 = (f32[8,128]{1,0:T(8,128)S(1)}, f32[8,128]{1,0:T(8,128)S(1)}, u32[]{:S(2)}, u32[]{:S(2)}) collective-permute-start(f32[8,128]{1,0:T(8,128)S(1)} %add.62), channel_id=1, source_target_pairs={{32,64},{64,32},{96,0},{0,96},{33,65},{65,33},{97,1},{1,97},{34,66... | collective-permute-start | bytes 12296 | tf_op jit(solution)/shard_map/ppermute | solution.py:499
  140.7 3.0 %collective-permute-done.21 = f32[8,128]{1,0:T(8,128)S(1)} collective-permute-done((f32[8,128]{1,0:T(8,128)S(1)}, f32[8,128]{1,0:T(8,128)S(1)}, u32[]{:S(2)}, u32[]{:S(2)}) %collective-permute-start.21) | collective-permute-done | bytes 4128 | tf_op jit(solution)/shard_map/ppermute | solution.py:499
  143.7 3.0 %finish.1 = (f32[512,512]{1,0:T(8,128)}, f32[512,512]{1,0:T(8,128)}) custom-call(s32[2]{0:T(128)S(1)} %pad_add_fusion.1.place, f32[8,128]{1,0:T(8,128)S(1)} %add.56.sums_in.sums_one, f32[8,128]{1,0:T(8,128)S(1)} %add.63.sums_two, f32[544,640]{1,0:T(8,128)S(1)} %get-tuple-element.47.own_in, f32[32,640]{1,0:T(8,128)S(1)} %collective-permute-done.22.first_in.rim_l, ...), custom_call_target="tpu_custom_call" | custom-call | tf_op jit(solution)/shard_map/finish/pallas_call | solution.py:457
  (31 shorter events, 0.4 us)
Async XLA Ops:
  5.3 29.0 %all-to-all-start = ((bf16[16,2,160,128]{3,2,1,0:T(8,128)(2,1)}), bf16[16,2,160,128]{3,2,1,0:T(8,128)(2,1)S(1)}, u32[]{:S(2)}, u32[]{:S(2)}) async-start(bf16[16,2,160,128]{3,2,1,0:T(8,128)(2,1)} %bitcast.10), calls=%async_computation | async-start | bytes 2621440 | tf_op jit(solution)/shard_map/all_to_all | solution.py:541
  41.3 4.5 %collective-permute-start = (f32[32,640]{1,0:T(8,128)S(1)}, f32[32,640]{1,0:T(8,128)S(1)}, u32[]{:S(2)}, u32[]{:S(2)}) collective-permute-start(f32[32,640]{1,0:T(8,128)S(1)} %get-tuple-element.30), channel_id=1, source_target_pairs={{0,1},{1,0},{2,3},{3,2},{4,5},{5,4},{6,7},{7,6},{8,9},{9,8},{10,11... | collective-permute-start | bytes 245768 | tf_op jit(solution)/shard_map/ppermute | solution.py:494
  41.4 7.8 %collective-permute-start.1 = (f32[32,640]{1,0:T(8,128)S(1)}, f32[32,640]{1,0:T(8,128)S(1)}, u32[]{:S(2)}, u32[]{:S(2)}) collective-permute-start(f32[32,640]{1,0:T(8,128)S(1)} %get-tuple-element.31), channel_id=1, source_target_pairs={{1,2},{2,1},{3,4},{4,3},{5,6},{6,5},{7,8},{8,7},{9,10},{10,9},{11,... | collective-permute-start | bytes 245768 | tf_op jit(solution)/shard_map/ppermute | solution.py:494
  49.8 2.2 %collective-permute-start.2 = (f32[32,640]{1,0:T(8,128)S(1)}, f32[32,640]{1,0:T(8,128)S(1)}, u32[]{:S(2)}, u32[]{:S(2)}) collective-permute-start(f32[32,640]{1,0:T(8,128)S(1)} %get-tuple-element.34), channel_id=1, source_target_pairs={{0,16},{16,0},{32,48},{48,32},{64,80},{80,64},{96,112},{112,96},{1... | collective-permute-start | bytes 245768 | tf_op jit(solution)/shard_map/ppermute | solution.py:494
  49.9 5.2 %collective-permute-start.3 = (f32[32,640]{1,0:T(8,128)S(1)}, f32[32,640]{1,0:T(8,128)S(1)}, u32[]{:S(2)}, u32[]{:S(2)}) collective-permute-start(f32[32,640]{1,0:T(8,128)S(1)} %get-tuple-element.35), channel_id=1, source_target_pairs={{16,32},{32,16},{48,64},{64,48},{80,96},{96,80},{0,112},{112,0},{1... | collective-permute-start | bytes 245768 | tf_op jit(solution)/shard_map/ppermute | solution.py:494
  66.3 12.3 %collective-permute-start.11 = (f32[32,640]{1,0:T(8,128)S(1)}, f32[32,640]{1,0:T(8,128)S(1)}, u32[]{:S(2)}, u32[]{:S(2)}) collective-permute-start(f32[32,640]{1,0:T(8,128)S(1)} %get-tuple-element.39), channel_id=1, source_target_pairs={{0,1},{1,0},{2,3},{3,2},{4,5},{5,4},{6,7},{7,6},{8,9},{9,8},{10,11... | collective-permute-start | bytes 245768 | tf_op jit(solution)/shard_map/ppermute | solution.py:494
  66.4 12.2 %collective-permute-start.12 = (f32[32,640]{1,0:T(8,128)S(1)}, f32[32,640]{1,0:T(8,128)S(1)}, u32[]{:S(2)}, u32[]{:S(2)}) collective-permute-start(f32[32,640]{1,0:T(8,128)S(1)} %get-tuple-element.40), channel_id=1, source_target_pairs={{1,2},{2,1},{3,4},{4,3},{5,6},{6,5},{7,8},{8,7},{9,10},{10,9},{11,... | collective-permute-start | bytes 245768 | tf_op jit(solution)/shard_map/ppermute | solution.py:494
  66.5 7.3 %collective-permute-start.4 = (f32[8,128]{1,0:T(8,128)S(1)}, f32[8,128]{1,0:T(8,128)S(1)}, u32[]{:S(2)}, u32[]{:S(2)}) collective-permute-start(f32[8,128]{1,0:T(8,128)S(1)} %get-tuple-element.37), channel_id=1, source_target_pairs={{0,1},{1,0},{2,3},{3,2},{4,5},{5,4},{6,7},{7,6},{8,9},{9,8},{10,11... | collective-permute-start | bytes 12296 | tf_op jit(solution)/shard_map/ppermute | solution.py:498
  73.8 4.8 %collective-permute-start.5 = (f32[8,128]{1,0:T(8,128)S(1)}, f32[8,128]{1,0:T(8,128)S(1)}, u32[]{:S(2)}, u32[]{:S(2)}) collective-permute-start(f32[8,128]{1,0:T(8,128)S(1)} %add.50), channel_id=1, source_target_pairs={{1,2},{2,1},{3,0},{0,3},{5,6},{6,5},{7,4},{4,7},{9,10},{10,9},{11,... | collective-permute-start | bytes 12296 | tf_op jit(solution)/shard_map/ppermute | solution.py:499
  79.3 21.0 %collective-permute-start.13 = (f32[32,640]{1,0:T(8,128)S(1)}, f32[32,640]{1,0:T(8,128)S(1)}, u32[]{:S(2)}, u32[]{:S(2)}) collective-permute-start(f32[32,640]{1,0:T(8,128)S(1)} %get-tuple-element.43), channel_id=1, source_target_pairs={{0,16},{16,0},{32,48},{48,32},{64,80},{80,64},{96,112},{112,96},{1... | collective-permute-start | bytes 245768 | tf_op jit(solution)/shard_map/ppermute | solution.py:494
  79.4 20.9 %collective-permute-start.14 = (f32[32,640]{1,0:T(8,128)S(1)}, f32[32,640]{1,0:T(8,128)S(1)}, u32[]{:S(2)}, u32[]{:S(2)}) collective-permute-start(f32[32,640]{1,0:T(8,128)S(1)} %get-tuple-element.44), channel_id=1, source_target_pairs={{16,32},{32,16},{48,64},{64,48},{80,96},{96,80},{0,112},{112,0},{1... | collective-permute-start | bytes 245768 | tf_op jit(solution)/shard_map/ppermute | solution.py:494
  80.2 1.2 collective-permute-start.6
  81.4 5.6 %collective-permute-start.7 = (f32[8,128]{1,0:T(8,128)S(1)}, f32[8,128]{1,0:T(8,128)S(1)}, u32[]{:S(2)}, u32[]{:S(2)}) collective-permute-start(f32[8,128]{1,0:T(8,128)S(1)} %add.52), channel_id=1, source_target_pairs={{0,4},{4,0},{8,12},{12,8},{1,5},{5,1},{9,13},{13,9},{2,6},{6,2},{1... | collective-permute-start | bytes 12296 | tf_op jit(solution)/shard_map/ppermute | solution.py:498
  87.0 4.8 %collective-permute-start.8 = (f32[8,128]{1,0:T(8,128)S(1)}, f32[8,128]{1,0:T(8,128)S(1)}, u32[]{:S(2)}, u32[]{:S(2)}) collective-permute-start(f32[8,128]{1,0:T(8,128)S(1)} %add.53), channel_id=1, source_target_pairs={{4,8},{8,4},{12,0},{0,12},{5,9},{9,5},{13,1},{1,13},{6,10},{10,6},... | collective-permute-start | bytes 12296 | tf_op jit(solution)/shard_map/ppermute | solution.py:499
  91.8 3.6 %collective-permute-start.9 = (f32[8,128]{1,0:T(8,128)S(1)}, f32[8,128]{1,0:T(8,128)S(1)}, u32[]{:S(2)}, u32[]{:S(2)}) collective-permute-start(f32[8,128]{1,0:T(8,128)S(1)} %add.54), channel_id=1, source_target_pairs={{0,32},{32,0},{64,96},{96,64},{1,33},{33,1},{65,97},{97,65},{2,34}... | collective-permute-start | bytes 12296 | tf_op jit(solution)/shard_map/ppermute | solution.py:498
  95.4 4.8 %collective-permute-start.10 = (f32[8,128]{1,0:T(8,128)S(1)}, f32[8,128]{1,0:T(8,128)S(1)}, u32[]{:S(2)}, u32[]{:S(2)}) collective-permute-start(f32[8,128]{1,0:T(8,128)S(1)} %add.55), channel_id=1, source_target_pairs={{32,64},{64,32},{96,0},{0,96},{33,65},{65,33},{97,1},{1,97},{34,66... | collective-permute-start | bytes 12296 | tf_op jit(solution)/shard_map/ppermute | solution.py:499
  112.0 9.6 %collective-permute-start.22 = (f32[32,640]{1,0:T(8,128)S(1)}, f32[32,640]{1,0:T(8,128)S(1)}, u32[]{:S(2)}, u32[]{:S(2)}) collective-permute-start(f32[32,640]{1,0:T(8,128)S(1)} %get-tuple-element.48), channel_id=1, source_target_pairs={{0,1},{1,0},{2,3},{3,2},{4,5},{5,4},{6,7},{7,6},{8,9},{9,8},{10,11... | collective-permute-start | bytes 245768 | tf_op jit(solution)/shard_map/ppermute | solution.py:494
  112.1 9.5 %collective-permute-start.23 = (f32[32,640]{1,0:T(8,128)S(1)}, f32[32,640]{1,0:T(8,128)S(1)}, u32[]{:S(2)}, u32[]{:S(2)}) collective-permute-start(f32[32,640]{1,0:T(8,128)S(1)} %get-tuple-element.49), channel_id=1, source_target_pairs={{1,2},{2,1},{3,4},{4,3},{5,6},{6,5},{7,8},{8,7},{9,10},{10,9},{11,... | collective-permute-start | bytes 245768 | tf_op jit(solution)/shard_map/ppermute | solution.py:494
  112.2 4.6 %collective-permute-start.15 = (f32[8,128]{1,0:T(8,128)S(1)}, f32[8,128]{1,0:T(8,128)S(1)}, u32[]{:S(2)}, u32[]{:S(2)}) collective-permute-start(f32[8,128]{1,0:T(8,128)S(1)} %get-tuple-element.46), channel_id=1, source_target_pairs={{0,1},{1,0},{2,3},{3,2},{4,5},{5,4},{6,7},{7,6},{8,9},{9,8},{10,11... | collective-permute-start | bytes 12296 | tf_op jit(solution)/shard_map/ppermute | solution.py:498
  116.8 4.8 %collective-permute-start.16 = (f32[8,128]{1,0:T(8,128)S(1)}, f32[8,128]{1,0:T(8,128)S(1)}, u32[]{:S(2)}, u32[]{:S(2)}) collective-permute-start(f32[8,128]{1,0:T(8,128)S(1)} %add.57), channel_id=1, source_target_pairs={{1,2},{2,1},{3,0},{0,3},{5,6},{6,5},{7,4},{4,7},{9,10},{10,9},{11,... | collective-permute-start | bytes 12296 | tf_op jit(solution)/shard_map/ppermute | solution.py:499
  122.3 21.4 %collective-permute-start.24 = (f32[32,640]{1,0:T(8,128)S(1)}, f32[32,640]{1,0:T(8,128)S(1)}, u32[]{:S(2)}, u32[]{:S(2)}) collective-permute-start(f32[32,640]{1,0:T(8,128)S(1)} %get-tuple-element.52), channel_id=1, source_target_pairs={{0,16},{16,0},{32,48},{48,32},{64,80},{80,64},{96,112},{112,96},{1... | collective-permute-start | bytes 245768 | tf_op jit(solution)/shard_map/ppermute | solution.py:494
  122.4 21.3 %collective-permute-start.25 = (f32[32,640]{1,0:T(8,128)S(1)}, f32[32,640]{1,0:T(8,128)S(1)}, u32[]{:S(2)}, u32[]{:S(2)}) collective-permute-start(f32[32,640]{1,0:T(8,128)S(1)} %get-tuple-element.53), channel_id=1, source_target_pairs={{16,32},{32,16},{48,64},{64,48},{80,96},{96,80},{0,112},{112,0},{1... | collective-permute-start | bytes 245768 | tf_op jit(solution)/shard_map/ppermute | solution.py:494
  123.6 1.2 collective-permute-start.17
  124.8 5.6 %collective-permute-start.18 = (f32[8,128]{1,0:T(8,128)S(1)}, f32[8,128]{1,0:T(8,128)S(1)}, u32[]{:S(2)}, u32[]{:S(2)}) collective-permute-start(f32[8,128]{1,0:T(8,128)S(1)} %add.59), channel_id=1, source_target_pairs={{0,4},{4,0},{8,12},{12,8},{1,5},{5,1},{9,13},{13,9},{2,6},{6,2},{1... | collective-permute-start | bytes 12296 | tf_op jit(solution)/shard_map/ppermute | solution.py:498
  130.4 4.8 %collective-permute-start.19 = (f32[8,128]{1,0:T(8,128)S(1)}, f32[8,128]{1,0:T(8,128)S(1)}, u32[]{:S(2)}, u32[]{:S(2)}) collective-permute-start(f32[8,128]{1,0:T(8,128)S(1)} %add.60), channel_id=1, source_target_pairs={{4,8},{8,4},{12,0},{0,12},{5,9},{9,5},{13,1},{1,13},{6,10},{10,6},... | collective-permute-start | bytes 12296 | tf_op jit(solution)/shard_map/ppermute | solution.py:499
  135.2 3.6 %collective-permute-start.20 = (f32[8,128]{1,0:T(8,128)S(1)}, f32[8,128]{1,0:T(8,128)S(1)}, u32[]{:S(2)}, u32[]{:S(2)}) collective-permute-start(f32[8,128]{1,0:T(8,128)S(1)} %add.61), channel_id=1, source_target_pairs={{0,32},{32,0},{64,96},{96,64},{1,33},{33,1},{65,97},{97,65},{2,34}... | collective-permute-start | bytes 12296 | tf_op jit(solution)/shard_map/ppermute | solution.py:498
  138.8 4.8 %collective-permute-start.21 = (f32[8,128]{1,0:T(8,128)S(1)}, f32[8,128]{1,0:T(8,128)S(1)}, u32[]{:S(2)}, u32[]{:S(2)}) collective-permute-start(f32[8,128]{1,0:T(8,128)S(1)} %add.62), channel_id=1, source_target_pairs={{32,64},{64,32},{96,0},{0,96},{33,65},{65,33},{97,1},{1,97},{34,66... | collective-permute-start | bytes 12296 | tf_op jit(solution)/shard_map/ppermute | solution.py:499
